TPU v7x, 128 devices: a whole 4x4x4 slice. The times are simulated.
128 devices in a mesh: lsec: 8 (over y, core), rsec: 16 (over x, z).
Axes of the slice: x: 4, y: 4, z: 4, core: 2. Of those that a mesh axis runs over, the one named last changes fastest.
Arguments:
- two_site: bfloat16 [2, 32, 128, 8192], P(None, 'lsec', None, 'rsec'), may hold values from -6 to 6
- left_env: bfloat16 [34, 32, 128, 128], P(None, 'lsec', 'rsec'), may hold values from -0.09375 to 0.09375
- right_env: bfloat16 [34, 64, 128, 128], P(None, 'rsec', 'lsec'), may hold values from -0.5 to 0.5
- left_size: int32 [32], P('lsec'), may hold values from 16 to 128, as said below
- right_size: int32 [64], P('rsec'), may hold values from 16 to 128, as said below
- channel_shift: int32 [34, 2], replicated, may hold values from -2 to 2, as said below
Outputs:
- applied: bfloat16 [2, 32, 128, 8192], P(None, 'lsec', None, 'rsec')
Inputs may be any that keep to these rules, and one draw needn't show every extreme that they name: `left_size`: each sector holds 16 to 128 states; some left sector and some right sector hold exactly 128. `right_size`: as for left_size. `channel_shift`: every offset from -2 to 2 is the left offset of some channel and the right offset of some channel.
All inputs are finite; a program needn't handle non-finite values.
Results may differ from a plain program's by a relative error of at most 0.0049.
Values may be sent and summed in bfloat16 or wider, within the bound.
No kernel may reach another device: no remote copies, remote signals or barrier semaphores. Data moves between devices by JAX's collectives and lax.ppermute only.
A program may use at most 64 MiB of HBM per device.

v0:
```python
import jax
import jax.numpy as jnp
from jax import lax
from jax.sharding import PartitionSpec as P

KCH = 34
SHIFT = 2


def with_halo(value, sides, width):
    for axis, dim in sides:
        devices, length = (lax.axis_size(axis), value.shape[dim])
        up = [(i, (i + 1) % devices) for i in range(devices - 1)]
        down = [(j, i) for i, j in up]
        last = lax.slice_in_dim(value, length - width, length, axis=dim)
        first = lax.slice_in_dim(value, 0, width, axis=dim)
        before = lax.ppermute(last, axis, up)
        after = lax.ppermute(first, axis, down)
        value = jnp.concatenate([before, value, after], axis=dim)
    return value


def live_states(sizes, padded_extent):
    states = jnp.arange(padded_extent, dtype=jnp.int32)
    return (states[None, :] < sizes[:, None]).reshape(sizes.shape[0] * padded_extent)


def local(two_site, left_env, right_env, left_size, right_size, channel_shift):
    vectors, left_count, padded_extent, columns = two_site.shape
    right_count = columns // padded_extent
    row_live = live_states(left_size, padded_extent)
    col_live = live_states(right_size, padded_extent)
    weights = (row_live[:, None] & col_live[None, :]).astype(jnp.bfloat16)
    masked = two_site.reshape(vectors, left_count * padded_extent, columns) * weights[None]
    rim_width = SHIFT * padded_extent
    enlarged_operand = with_halo(masked, (("lsec", 1), ("rsec", 2)), rim_width)
    right_whole = lax.all_gather(right_env, "lsec", axis=2, tiled=True)

    def left_blocks(channel):
        own_piece = lax.dynamic_index_in_dim(left_env, channel, 0, keepdims=False)
        return lax.all_gather(own_piece, "rsec", axis=1, tiled=True)

    row_count = left_count * padded_extent

    def one_channel(channel, cumulative_sum):
        row_start = (SHIFT - channel_shift[channel, 0]) * padded_extent
        col_start = (SHIFT - channel_shift[channel, 1]) * padded_extent
        source = lax.dynamic_slice(
            enlarged_operand, (jnp.int32(0), row_start, col_start), (vectors, row_count, columns)
        )
        source = source.reshape(vectors, left_count, padded_extent, right_count, padded_extent)
        right_block = lax.dynamic_index_in_dim(right_whole, channel, 0, keepdims=False)
        right_reduced = jnp.einsum(
            "vlarb,rcb->vlarc", source, right_block, preferred_element_type=jnp.float32
        ).astype(jnp.bfloat16)
        left_sector_tensor = left_blocks(channel)
        return cumulative_sum + jnp.einsum(
            "jit,xjtum->xjium",
            left_sector_tensor,
            right_reduced,
            preferred_element_type=jnp.float32,
        )

    start_total = jnp.zeros(
        (vectors, left_count, padded_extent, right_count, padded_extent), jnp.float32
    )
    total = lax.fori_loop(0, KCH, one_channel, start_total)
    total = total.reshape(vectors, row_count, columns)
    row_float = row_live.astype(jnp.float32)
    col_float = col_live.astype(jnp.float32)
    result = (total * row_float[None, :, None] * col_float[None, None, :]).astype(jnp.bfloat16)
    return result.reshape(vectors, left_count, padded_extent, columns)


def solution(mesh):
    placed = (
        P(None, "lsec", None, "rsec"),
        P(None, "lsec", "rsec", None),
        P(None, "rsec", "lsec", None),
        P("lsec"),
        P("rsec"),
        P(),
    )
    return jax.shard_map(
        local, mesh=mesh, in_specs=placed, out_specs=P(None, "lsec", None, "rsec"), check_vma=False
    )
```

profile of v0, /device:TPU:16, one launch (start us, length us, event | category | flops | bytes accessed | tf_op | source)
XLA Modules:
  0.0 1099.7 jit_solution(13334216231634703980)
XLA Ops:
  61.0 1028.7 %while.14 = (s32[]{:T(128)}, f32[2,4,128,4,128]{2,4,3,0,1:T(8,128)}, bf16[34,4,128,128]{3,2,1,0:T(8,128)(2,1)}, s32[34,2]{0,1:T(2,128)S(1)}, bf16[2,1024,1024]{2...) while((s32[]{:T(128)}, ...), condition=%wide.region_1.2_spmd.clone, body=%wide.region_0.1_spmd.clone.sunk | while | flops 270008320 | bytes 9855755 | solution.py:67
  65.2 25.4 %all-gather.3 = bf16[1,4,128,128]{3,2,1,0:T(8,128)(2,1)S(1)} all-gather(bf16[1,4,8,128]{3,2,1,0:T(8,128)(2,1)S(1)} %constant_dynamic-slice_fusion.9), channel_id=2, replica_groups=mesh['lsec'=8,'rsec'=16] {'rsec'}, dimensions={2}, use_global_device_ids=true | all-gather | bytes 139264 | tf_op jit(solution)/shard_map/while/body/eval_jaxpr/all_gather | solution.py:41
  97.9 21.7 %all-gather.3 = bf16[1,4,128,128]{3,2,1,0:T(8,128)(2,1)S(1)} all-gather(bf16[1,4,8,128]{3,2,1,0:T(8,128)(2,1)S(1)} %constant_dynamic-slice_fusion.9), channel_id=2, replica_groups=mesh['lsec'=8,'rsec'=16] {'rsec'}, dimensions={2}, use_global_device_ids=true | all-gather | bytes 139264 | tf_op jit(solution)/shard_map/while/body/eval_jaxpr/all_gather | solution.py:41
  127.6 22.7 %all-gather.3 = bf16[1,4,128,128]{3,2,1,0:T(8,128)(2,1)S(1)} all-gather(bf16[1,4,8,128]{3,2,1,0:T(8,128)(2,1)S(1)} %constant_dynamic-slice_fusion.9), channel_id=2, replica_groups=mesh['lsec'=8,'rsec'=16] {'rsec'}, dimensions={2}, use_global_device_ids=true | all-gather | bytes 139264 | tf_op jit(solution)/shard_map/while/body/eval_jaxpr/all_gather | solution.py:41
  158.3 21.7 %all-gather.3 = bf16[1,4,128,128]{3,2,1,0:T(8,128)(2,1)S(1)} all-gather(bf16[1,4,8,128]{3,2,1,0:T(8,128)(2,1)S(1)} %constant_dynamic-slice_fusion.9), channel_id=2, replica_groups=mesh['lsec'=8,'rsec'=16] {'rsec'}, dimensions={2}, use_global_device_ids=true | all-gather | bytes 139264 | tf_op jit(solution)/shard_map/while/body/eval_jaxpr/all_gather | solution.py:41
  188.0 22.7 %all-gather.3 = bf16[1,4,128,128]{3,2,1,0:T(8,128)(2,1)S(1)} all-gather(bf16[1,4,8,128]{3,2,1,0:T(8,128)(2,1)S(1)} %constant_dynamic-slice_fusion.9), channel_id=2, replica_groups=mesh['lsec'=8,'rsec'=16] {'rsec'}, dimensions={2}, use_global_device_ids=true | all-gather | bytes 139264 | tf_op jit(solution)/shard_map/while/body/eval_jaxpr/all_gather | solution.py:41
  218.7 21.7 %all-gather.3 = bf16[1,4,128,128]{3,2,1,0:T(8,128)(2,1)S(1)} all-gather(bf16[1,4,8,128]{3,2,1,0:T(8,128)(2,1)S(1)} %constant_dynamic-slice_fusion.9), channel_id=2, replica_groups=mesh['lsec'=8,'rsec'=16] {'rsec'}, dimensions={2}, use_global_device_ids=true | all-gather | bytes 139264 | tf_op jit(solution)/shard_map/while/body/eval_jaxpr/all_gather | solution.py:41
  248.4 22.6 %all-gather.3 = bf16[1,4,128,128]{3,2,1,0:T(8,128)(2,1)S(1)} all-gather(bf16[1,4,8,128]{3,2,1,0:T(8,128)(2,1)S(1)} %constant_dynamic-slice_fusion.9), channel_id=2, replica_groups=mesh['lsec'=8,'rsec'=16] {'rsec'}, dimensions={2}, use_global_device_ids=true | all-gather | bytes 139264 | tf_op jit(solution)/shard_map/while/body/eval_jaxpr/all_gather | solution.py:41
  279.1 21.7 %all-gather.3 = bf16[1,4,128,128]{3,2,1,0:T(8,128)(2,1)S(1)} all-gather(bf16[1,4,8,128]{3,2,1,0:T(8,128)(2,1)S(1)} %constant_dynamic-slice_fusion.9), channel_id=2, replica_groups=mesh['lsec'=8,'rsec'=16] {'rsec'}, dimensions={2}, use_global_device_ids=true | all-gather | bytes 139264 | tf_op jit(solution)/shard_map/while/body/eval_jaxpr/all_gather | solution.py:41
  308.8 22.7 %all-gather.3 = bf16[1,4,128,128]{3,2,1,0:T(8,128)(2,1)S(1)} all-gather(bf16[1,4,8,128]{3,2,1,0:T(8,128)(2,1)S(1)} %constant_dynamic-slice_fusion.9), channel_id=2, replica_groups=mesh['lsec'=8,'rsec'=16] {'rsec'}, dimensions={2}, use_global_device_ids=true | all-gather | bytes 139264 | tf_op jit(solution)/shard_map/while/body/eval_jaxpr/all_gather | solution.py:41
  369.2 22.7 %all-gather.3 = bf16[1,4,128,128]{3,2,1,0:T(8,128)(2,1)S(1)} all-gather(bf16[1,4,8,128]{3,2,1,0:T(8,128)(2,1)S(1)} %constant_dynamic-slice_fusion.9), channel_id=2, replica_groups=mesh['lsec'=8,'rsec'=16] {'rsec'}, dimensions={2}, use_global_device_ids=true | all-gather | bytes 139264 | tf_op jit(solution)/shard_map/while/body/eval_jaxpr/all_gather | solution.py:41
  399.9 21.7 %all-gather.3 = bf16[1,4,128,128]{3,2,1,0:T(8,128)(2,1)S(1)} all-gather(bf16[1,4,8,128]{3,2,1,0:T(8,128)(2,1)S(1)} %constant_dynamic-slice_fusion.9), channel_id=2, replica_groups=mesh['lsec'=8,'rsec'=16] {'rsec'}, dimensions={2}, use_global_device_ids=true | all-gather | bytes 139264 | tf_op jit(solution)/shard_map/while/body/eval_jaxpr/all_gather | solution.py:41
  429.6 22.7 %all-gather.3 = bf16[1,4,128,128]{3,2,1,0:T(8,128)(2,1)S(1)} all-gather(bf16[1,4,8,128]{3,2,1,0:T(8,128)(2,1)S(1)} %constant_dynamic-slice_fusion.9), channel_id=2, replica_groups=mesh['lsec'=8,'rsec'=16] {'rsec'}, dimensions={2}, use_global_device_ids=true | all-gather | bytes 139264 | tf_op jit(solution)/shard_map/while/body/eval_jaxpr/all_gather | solution.py:41
  460.3 21.7 %all-gather.3 = bf16[1,4,128,128]{3,2,1,0:T(8,128)(2,1)S(1)} all-gather(bf16[1,4,8,128]{3,2,1,0:T(8,128)(2,1)S(1)} %constant_dynamic-slice_fusion.9), channel_id=2, replica_groups=mesh['lsec'=8,'rsec'=16] {'rsec'}, dimensions={2}, use_global_device_ids=true | all-gather | bytes 139264 | tf_op jit(solution)/shard_map/while/body/eval_jaxpr/all_gather | solution.py:41
  490.0 22.7 %all-gather.3 = bf16[1,4,128,128]{3,2,1,0:T(8,128)(2,1)S(1)} all-gather(bf16[1,4,8,128]{3,2,1,0:T(8,128)(2,1)S(1)} %constant_dynamic-slice_fusion.9), channel_id=2, replica_groups=mesh['lsec'=8,'rsec'=16] {'rsec'}, dimensions={2}, use_global_device_ids=true | all-gather | bytes 139264 | tf_op jit(solution)/shard_map/while/body/eval_jaxpr/all_gather | solution.py:41
  520.7 21.7 %all-gather.3 = bf16[1,4,128,128]{3,2,1,0:T(8,128)(2,1)S(1)} all-gather(bf16[1,4,8,128]{3,2,1,0:T(8,128)(2,1)S(1)} %constant_dynamic-slice_fusion.9), channel_id=2, replica_groups=mesh['lsec'=8,'rsec'=16] {'rsec'}, dimensions={2}, use_global_device_ids=true | all-gather | bytes 139264 | tf_op jit(solution)/shard_map/while/body/eval_jaxpr/all_gather | solution.py:41
  550.4 22.7 %all-gather.3 = bf16[1,4,128,128]{3,2,1,0:T(8,128)(2,1)S(1)} all-gather(bf16[1,4,8,128]{3,2,1,0:T(8,128)(2,1)S(1)} %constant_dynamic-slice_fusion.9), channel_id=2, replica_groups=mesh['lsec'=8,'rsec'=16] {'rsec'}, dimensions={2}, use_global_device_ids=true | all-gather | bytes 139264 | tf_op jit(solution)/shard_map/while/body/eval_jaxpr/all_gather | solution.py:41
  581.1 21.7 %all-gather.3 = bf16[1,4,128,128]{3,2,1,0:T(8,128)(2,1)S(1)} all-gather(bf16[1,4,8,128]{3,2,1,0:T(8,128)(2,1)S(1)} %constant_dynamic-slice_fusion.9), channel_id=2, replica_groups=mesh['lsec'=8,'rsec'=16] {'rsec'}, dimensions={2}, use_global_device_ids=true | all-gather | bytes 139264 | tf_op jit(solution)/shard_map/while/body/eval_jaxpr/all_gather | solution.py:41
  610.8 22.7 %all-gather.3 = bf16[1,4,128,128]{3,2,1,0:T(8,128)(2,1)S(1)} all-gather(bf16[1,4,8,128]{3,2,1,0:T(8,128)(2,1)S(1)} %constant_dynamic-slice_fusion.9), channel_id=2, replica_groups=mesh['lsec'=8,'rsec'=16] {'rsec'}, dimensions={2}, use_global_device_ids=true | all-gather | bytes 139264 | tf_op jit(solution)/shard_map/while/body/eval_jaxpr/all_gather | solution.py:41
  641.5 21.7 %all-gather.3 = bf16[1,4,128,128]{3,2,1,0:T(8,128)(2,1)S(1)} all-gather(bf16[1,4,8,128]{3,2,1,0:T(8,128)(2,1)S(1)} %constant_dynamic-slice_fusion.9), channel_id=2, replica_groups=mesh['lsec'=8,'rsec'=16] {'rsec'}, dimensions={2}, use_global_device_ids=true | all-gather | bytes 139264 | tf_op jit(solution)/shard_map/while/body/eval_jaxpr/all_gather | solution.py:41
  671.2 22.7 %all-gather.3 = bf16[1,4,128,128]{3,2,1,0:T(8,128)(2,1)S(1)} all-gather(bf16[1,4,8,128]{3,2,1,0:T(8,128)(2,1)S(1)} %constant_dynamic-slice_fusion.9), channel_id=2, replica_groups=mesh['lsec'=8,'rsec'=16] {'rsec'}, dimensions={2}, use_global_device_ids=true | all-gather | bytes 139264 | tf_op jit(solution)/shard_map/while/body/eval_jaxpr/all_gather | solution.py:41
  701.9 21.7 %all-gather.3 = bf16[1,4,128,128]{3,2,1,0:T(8,128)(2,1)S(1)} all-gather(bf16[1,4,8,128]{3,2,1,0:T(8,128)(2,1)S(1)} %constant_dynamic-slice_fusion.9), channel_id=2, replica_groups=mesh['lsec'=8,'rsec'=16] {'rsec'}, dimensions={2}, use_global_device_ids=true | all-gather | bytes 139264 | tf_op jit(solution)/shard_map/while/body/eval_jaxpr/all_gather | solution.py:41
  731.6 22.7 %all-gather.3 = bf16[1,4,128,128]{3,2,1,0:T(8,128)(2,1)S(1)} all-gather(bf16[1,4,8,128]{3,2,1,0:T(8,128)(2,1)S(1)} %constant_dynamic-slice_fusion.9), channel_id=2, replica_groups=mesh['lsec'=8,'rsec'=16] {'rsec'}, dimensions={2}, use_global_device_ids=true | all-gather | bytes 139264 | tf_op jit(solution)/shard_map/while/body/eval_jaxpr/all_gather | solution.py:41
  762.3 21.7 %all-gather.3 = bf16[1,4,128,128]{3,2,1,0:T(8,128)(2,1)S(1)} all-gather(bf16[1,4,8,128]{3,2,1,0:T(8,128)(2,1)S(1)} %constant_dynamic-slice_fusion.9), channel_id=2, replica_groups=mesh['lsec'=8,'rsec'=16] {'rsec'}, dimensions={2}, use_global_device_ids=true | all-gather | bytes 139264 | tf_op jit(solution)/shard_map/while/body/eval_jaxpr/all_gather | solution.py:41
  792.0 22.7 %all-gather.3 = bf16[1,4,128,128]{3,2,1,0:T(8,128)(2,1)S(1)} all-gather(bf16[1,4,8,128]{3,2,1,0:T(8,128)(2,1)S(1)} %constant_dynamic-slice_fusion.9), channel_id=2, replica_groups=mesh['lsec'=8,'rsec'=16] {'rsec'}, dimensions={2}, use_global_device_ids=true | all-gather | bytes 139264 | tf_op jit(solution)/shard_map/while/body/eval_jaxpr/all_gather | solution.py:41
  822.6 21.7 %all-gather.3 = bf16[1,4,128,128]{3,2,1,0:T(8,128)(2,1)S(1)} all-gather(bf16[1,4,8,128]{3,2,1,0:T(8,128)(2,1)S(1)} %constant_dynamic-slice_fusion.9), channel_id=2, replica_groups=mesh['lsec'=8,'rsec'=16] {'rsec'}, dimensions={2}, use_global_device_ids=true | all-gather | bytes 139264 | tf_op jit(solution)/shard_map/while/body/eval_jaxpr/all_gather | solution.py:41
  852.4 22.7 %all-gather.3 = bf16[1,4,128,128]{3,2,1,0:T(8,128)(2,1)S(1)} all-gather(bf16[1,4,8,128]{3,2,1,0:T(8,128)(2,1)S(1)} %constant_dynamic-slice_fusion.9), channel_id=2, replica_groups=mesh['lsec'=8,'rsec'=16] {'rsec'}, dimensions={2}, use_global_device_ids=true | all-gather | bytes 139264 | tf_op jit(solution)/shard_map/while/body/eval_jaxpr/all_gather | solution.py:41
  912.8 22.7 %all-gather.3 = bf16[1,4,128,128]{3,2,1,0:T(8,128)(2,1)S(1)} all-gather(bf16[1,4,8,128]{3,2,1,0:T(8,128)(2,1)S(1)} %constant_dynamic-slice_fusion.9), channel_id=2, replica_groups=mesh['lsec'=8,'rsec'=16] {'rsec'}, dimensions={2}, use_global_device_ids=true | all-gather | bytes 139264 | tf_op jit(solution)/shard_map/while/body/eval_jaxpr/all_gather | solution.py:41
  973.1 22.7 %all-gather.3 = bf16[1,4,128,128]{3,2,1,0:T(8,128)(2,1)S(1)} all-gather(bf16[1,4,8,128]{3,2,1,0:T(8,128)(2,1)S(1)} %constant_dynamic-slice_fusion.9), channel_id=2, replica_groups=mesh['lsec'=8,'rsec'=16] {'rsec'}, dimensions={2}, use_global_device_ids=true | all-gather | bytes 139264 | tf_op jit(solution)/shard_map/while/body/eval_jaxpr/all_gather | solution.py:41
  1003.8 21.7 %all-gather.3 = bf16[1,4,128,128]{3,2,1,0:T(8,128)(2,1)S(1)} all-gather(bf16[1,4,8,128]{3,2,1,0:T(8,128)(2,1)S(1)} %constant_dynamic-slice_fusion.9), channel_id=2, replica_groups=mesh['lsec'=8,'rsec'=16] {'rsec'}, dimensions={2}, use_global_device_ids=true | all-gather | bytes 139264 | tf_op jit(solution)/shard_map/while/body/eval_jaxpr/all_gather | solution.py:41
  1033.5 22.7 %all-gather.3 = bf16[1,4,128,128]{3,2,1,0:T(8,128)(2,1)S(1)} all-gather(bf16[1,4,8,128]{3,2,1,0:T(8,128)(2,1)S(1)} %constant_dynamic-slice_fusion.9), channel_id=2, replica_groups=mesh['lsec'=8,'rsec'=16] {'rsec'}, dimensions={2}, use_global_device_ids=true | all-gather | bytes 139264 | tf_op jit(solution)/shard_map/while/body/eval_jaxpr/all_gather | solution.py:41
  1064.2 21.7 %all-gather.3 = bf16[1,4,128,128]{3,2,1,0:T(8,128)(2,1)S(1)} all-gather(bf16[1,4,8,128]{3,2,1,0:T(8,128)(2,1)S(1)} %constant_dynamic-slice_fusion.9), channel_id=2, replica_groups=mesh['lsec'=8,'rsec'=16] {'rsec'}, dimensions={2}, use_global_device_ids=true | all-gather | bytes 139264 | tf_op jit(solution)/shard_map/while/body/eval_jaxpr/all_gather | solution.py:41
  (197 shorter events, 349.8 us)
Async XLA Ops:
  6.5 54.4 %all-gather.6.cloned.1.call-start = ((), (), s32[]{:S(2)}) async-start(), calls=%async_computation | async-start | bytes 5013504 | tf_op jit(solution)/shard_map/all_gather | solution.py:37
  10.3 10.5 collective-permute-start
  12.2 11.3 %collective-permute-start.1 = (bf16[2,256,512]{2,1,0:T(8,128)(2,1)S(1)}, bf16[2,256,512]{2,1,0:T(8,128)(2,1)S(1)}, u32[]{:S(2)}, u32[]{:S(2)}) collective-permute-start(bf16[2,256,512]{2,1,0:T(8,128)(2,1)S(1)} %get-tuple-element.153), channel_id=1, source_target_pairs={{16,0},{32,16},{48,32},{64,48},{80,64},{96,80},{112,96},{17,1},{33... | collective-permute-start | bytes 1572872 | tf_op jit(solution)/shard_map/ppermute | solution.py:18
  24.8 27.2 %collective-permute-start.2 = (bf16[2,1024,256]{2,1,0:T(8,128)(2,1)}, bf16[2,1024,256]{2,1,0:T(8,128)(2,1)}, u32[]{:S(2)}, u32[]{:S(2)}) collective-permute-start(bf16[2,1024,256]{2,1,0:T(8,128)(2,1)} %get-tuple-element.150), channel_id=1, source_target_pairs={{0,1},{1,2},{2,3},{3,4},{4,5},{5,6},{6,7},{7,8},{8,9},{9,10},{10,1... | collective-permute-start | bytes 3145736 | tf_op jit(solution)/shard_map/ppermute | solution.py:17
  30.3 27.1 %collective-permute-start.3 = (bf16[2,1024,256]{2,1,0:T(8,128)(2,1)S(1)}, bf16[2,1024,256]{2,1,0:T(8,128)(2,1)}, u32[]{:S(2)}, u32[]{:S(2)}) collective-permute-start(bf16[2,1024,256]{2,1,0:T(8,128)(2,1)S(1)} %get-tuple-element.151), channel_id=1, source_target_pairs={{1,0},{2,1},{3,2},{4,3},{5,4},{6,5},{7,6},{8,7},{9,8},{10,9},{11,1... | collective-permute-start | bytes 3145736 | tf_op jit(solution)/shard_map/ppermute | solution.py:18
  31.6 29.3 %copy-start = (s32[34,2]{0,1:T(2,128)S(1)}, s32[34,2]{0,1:T(2,128)}, u32[]{:S(2)}) copy-start(s32[34,2]{0,1:T(2,128)} %param.13) | copy-start | bytes 820
Sparse Core Ops, SparseCore 0:
  9.0 38.4 all-gather.5
where the time goes:
time: 1110 us; the launch traced here: 1100 us
  blocking collectives  757 us (68%)
  matrix products  128 us (12%)
  local copies, waits for them, and re-layouts  102 us (9%)
  loops' own time  44.5 us (4%)
  waiting for transfers between devices  34.2 us (3%)
  between operations  13.5 us (1%)
  starting transfers between devices  12.4 us (1%)
    all_gather x34, blocking collectives, left_blocks(): return lax.all_gather(own_piece, 'rsec', axis=1, tiled=True)  757 us
    dot_general x34, matrix products, one_channel(): jnp.einsum('jit,xjtum->xjium', left_sector_tensor, right_reduced, preferr...  128 us
    dynamic_slice x34, local copies, waits for them, and re-layouts, one_channel(): lax.dynamic_slice(enlarged_operand, (jnp.int32(0), row_start, col_start),...  44.9 us
    another operation x1, loops' own time, local(): total = lax.fori_loop(0, KCH, one_channel, start_total)  44.5 us
    ppermute x2, waiting for transfers between devices, with_halo(): before = lax.ppermute(last, axis, up)  25.3 us
    dynamic_slice x34, local copies, waits for them, and re-layouts, left_blocks(): own_piece = lax.dynamic_index_in_dim(left_env, channel, 0, keepdims=False)  23.9 us
  transfers between devices with their start and end apart: 5, of which 4 were waited for; matrix products, arithmetic and copies ran while one was open for 1% of the time, Pallas kernels for 0%

commit v1 on v0

v1 whole, which is shorter than its diff:
```python
import functools

import jax
import jax.numpy as jnp
from jax import lax
from jax.experimental import pallas as pl
from jax.experimental.pallas import tpu as pltpu
from jax.sharding import PartitionSpec as P

KCH = 34
SHIFT = 2
SPLIT = 18
XN, ZN, YN, CORES = 4, 4, 4, 2
NT = (((1,), (1,)), ((), ()))
NN = (((1,), (0,)), ((), ()))


def shifted_x(step):
    return [(ZN * x + z, ZN * ((x + step) % XN) + z) for x in range(XN) for z in range(ZN)]


def shifted_z(step):
    return [(ZN * x + z, ZN * x + (z + step) % ZN) for x in range(XN) for z in range(ZN)]


def shifted_y(step):
    return [(CORES * y + c, CORES * ((y + step) % YN) + c) for y in range(YN) for c in range(CORES)]


def ring_of_four(value, axis, shifted):
    half = value.shape[0] // 2
    left = lax.ppermute(value, axis, shifted(1))
    right = lax.ppermute(value, axis, shifted(-1))
    far_a = lax.ppermute(left[:half], axis, shifted(1))
    far_b = lax.ppermute(right[half:], axis, shifted(-1))
    return left, right, far_a, far_b


def four_segments(count):
    half = count // 2
    return (
        (0, 0, count, 0),
        (count, 0, count, -1),
        (2 * count, 0, count, 1),
        (3 * count, 0, half, 2),
        (3 * count + half, half, half, 2),
    )


def bundle_segments(count):
    inner = four_segments(count)
    rows = 4 * count
    half = rows // 2
    found = []
    for row, start, many, step in inner:
        found.append((0, row, start, many, step, 0))
        found.append((1, row, start, many, step, -1))
        found.append((2, row, start, many, step, 1))
        if row < half:
            found.append((3, row, start, many, step, 2))
        else:
            found.append((4, row - half, start, many, step, 2))
    return tuple(found)


def live_states(sizes, padded_extent):
    states = jnp.arange(padded_extent, dtype=jnp.int32)
    return states[None, :] < sizes[:, None]


def channels_kernel(
    first, count, z_first, is_first, is_last,
    shift, left_size, right_size,
    own, low_l, high_l, low_r, high_r, lefts, rights, *rest,
):
    rest = list(rest)
    total_in = None if is_first else rest.pop(0)
    out = rest.pop(0)
    source, left_all, right_all = rest[:3]
    rest = rest[3:]
    if is_last:
        total = rest.pop(0)
    else:
        total = out
    sems = rest.pop(0)
    rsec, lsec = lax.axis_index("rsec"), lax.axis_index("lsec")
    x, z, y, core = rsec // ZN, lax.rem(rsec, ZN), lsec // CORES, lax.rem(lsec, CORES)

    copies = []

    def start(src, dst, which):
        copy = pltpu.make_async_copy(src, dst, sems.at[which])
        copy.start()
        copies.append(copy)

    start(own, source.at[2:6, 2:6], 0)
    start(low_l, source.at[2:6, 0:2], 1)
    start(high_l, source.at[2:6, 6:8], 2)
    start(low_r, source.at[0:2], 3)
    start(high_r, source.at[6:8], 4)
    at = 5
    for row, begin, many, step in four_segments(KCH):
        lo, hi = max(begin, first), min(begin + many, first + count)
        if hi <= lo:
            continue
        for which, side in ((0, core), (1, 1 - core)):
            rows = 16 * (CORES * lax.rem(y + step + YN, YN) + side)
            start(
                rights[which].at[row + lo - begin : row + hi - begin],
                right_all.at[lo - first : hi - first, :, pl.ds(pl.multiple_of(rows, 16), 16)],
                at,
            )
            at += 1
    for which, row, begin, many, inner, outer in bundle_segments(count):
        dx, dz = (outer, inner) if z_first else (inner, outer)
        rows = 8 * (ZN * lax.rem(x + dx + XN, XN) + lax.rem(z + dz + ZN, ZN))
        start(
            lefts[which].at[row : row + many],
            left_all.at[begin : begin + many, :, pl.ds(pl.multiple_of(rows, 8), 8)],
            at,
        )
        at += 1
    if is_first:
        total[...] = jnp.zeros_like(total)
    else:
        start(total_in, total, at)
    for copy in copies:
        copy.wait()

    def two_channels(pair, carry):
        ks = (2 * pair, 2 * pair + 1)
        shifts = [(shift[first + k, 0], shift[first + k, 1]) for k in ks]
        for r in range(4):
            partial = []
            for k, (dl, dr) in zip(ks, shifts):
                rows = source[r + SHIFT - dr, pl.ds(SHIFT - dl, 4)].reshape(4 * 256, 128)
                partial.append(
                    lax.dot_general(
                        rows, right_all[k, r], NT, preferred_element_type=jnp.float32
                    ).astype(jnp.bfloat16)
                )
            for l in range(4):
                stacked = jnp.concatenate(
                    [
                        jnp.concatenate(
                            [p[l * 256 : l * 256 + 128], p[l * 256 + 128 : l * 256 + 256]], axis=1
                        )
                        for p in partial
                    ],
                    axis=0,
                )
                sides = jnp.concatenate([left_all[k, l] for k in ks], axis=1)
                total[l, r] += lax.dot_general(
                    sides, stacked, NN, preferred_element_type=jnp.float32
                )
        return carry

    lax.fori_loop(0, count // 2, two_channels, 0)

    if is_last:
        row = lax.broadcasted_iota(jnp.int32, (128, 128), 0)
        col = lax.broadcasted_iota(jnp.int32, (128, 128), 1)
        for l in range(4):
            for r in range(4):
                live = (row < left_size[l]) & (col < right_size[r])
                for v in range(2):
                    block = total[l, r, :, v * 128 : v * 128 + 128]
                    out[v, l, :, r * 128 : r * 128 + 128] = jnp.where(live, block, 0.0).astype(
                        jnp.bfloat16
                    )


def run_channels(first, count, z_first, is_first, is_last, scalars, sources, lefts, rights, total):
    totals = jax.ShapeDtypeStruct((4, 4, 128, 256), jnp.float32)
    result = jax.ShapeDtypeStruct((2, 4, 128, 512), jnp.bfloat16)
    anywhere = pl.BlockSpec(memory_space=pl.ANY)
    smem = pl.BlockSpec(memory_space=pltpu.SMEM)
    operands = [*scalars, *sources, tuple(lefts), tuple(rights)]
    specs = [smem] * 3 + [anywhere] * 5 + [(anywhere,) * len(lefts), (anywhere,) * len(rights)]
    if not is_first:
        operands.append(total)
        specs.append(anywhere)
    scratch = [
        pltpu.VMEM((8, 8, 256, 128), jnp.bfloat16),
        pltpu.VMEM((count, 4, 128, 128), jnp.bfloat16),
        pltpu.VMEM((count, 4, 128, 128), jnp.bfloat16),
    ]
    if is_last:
        scratch.append(pltpu.VMEM((4, 4, 128, 256), jnp.float32))
    scratch.append(pltpu.SemaphoreType.DMA((64,)))
    return pl.pallas_call(
        functools.partial(channels_kernel, first, count, z_first, is_first, is_last),
        out_shape=result if is_last else totals,
        in_specs=specs,
        out_specs=pl.BlockSpec(memory_space=pltpu.VMEM),
        scratch_shapes=scratch,
        compiler_params=pltpu.CompilerParams(vmem_limit_bytes=32 << 20),
        cost_estimate=pl.CostEstimate(
            flops=count * 4 * 4 * 2 * 2 * 2 * 128**3, bytes_accessed=10 << 20, transcendentals=0
        ),
    )(*operands)


def local(two_site, left_env, right_env, left_size, right_size, channel_shift):
    row_live = live_states(left_size, 128)
    col_live = live_states(right_size, 128)
    blocks = two_site.reshape(2, 4, 128, 4, 128)
    live = row_live[None, :, :, None, None] & col_live[None, None, None, :, :]
    own = jnp.where(live, blocks, jnp.bfloat16(0)).transpose(3, 1, 0, 2, 4).reshape(4, 4, 256, 128)

    l_up = [(i, i + 1) for i in range(7)]
    l_down = [(i + 1, i) for i in range(7)]
    r_up = [(i, i + 1) for i in range(15)]
    r_down = [(i + 1, i) for i in range(15)]
    low_l = lax.ppermute(own[:, 2:], "lsec", l_up)
    high_l = lax.ppermute(own[:, :2], "lsec", l_down)
    low_r = lax.ppermute(
        jnp.concatenate([low_l[2:], own[2:], high_l[2:]], axis=1), "rsec", r_up
    )
    high_r = lax.ppermute(
        jnp.concatenate([low_l[:2], own[:2], high_l[:2]], axis=1), "rsec", r_down
    )

    y_bundle = jnp.concatenate([right_env, *ring_of_four(right_env, "lsec", shifted_y)], axis=0)
    partner = lax.ppermute(y_bundle, "lsec", [(i, i ^ 1) for i in range(8)])

    chunk_a = left_env[:SPLIT]
    chunk_b = left_env[SPLIT:]
    z_bundle = jnp.concatenate([chunk_a, *ring_of_four(chunk_a, "rsec", shifted_z)], axis=0)
    x_bundle = jnp.concatenate([chunk_b, *ring_of_four(chunk_b, "rsec", shifted_x)], axis=0)
    lefts_a = (z_bundle, *ring_of_four(z_bundle, "rsec", shifted_x))
    lefts_b = (x_bundle, *ring_of_four(x_bundle, "rsec", shifted_z))

    scalars = (channel_shift, left_size, right_size)
    sources = (own, low_l, high_l, low_r, high_r)
    rights = (y_bundle, partner)
    total = run_channels(0, SPLIT, True, True, False, scalars, sources, lefts_a, rights, None)
    return run_channels(
        SPLIT, KCH - SPLIT, False, False, True, scalars, sources, lefts_b, rights, total
    )


def solution(mesh):
    placed = (
        P(None, "lsec", None, "rsec"),
        P(None, "lsec", "rsec", None),
        P(None, "rsec", "lsec", None),
        P("lsec"),
        P("rsec"),
        P(),
    )
    return jax.shard_map(
        local, mesh=mesh, in_specs=placed, out_specs=P(None, "lsec", None, "rsec"), check_vma=False
    )
```

time: 1110 us -> 145 us (0.13)
  blocking collectives: 757 us -> 0 us
  matrix products: 128 us -> 0 us
  local copies, waits for them, and re-layouts: 102 us -> 22.9 us
  loops' own time: 44.5 us -> 0 us
  Pallas kernels: 0 us -> 32.5 us
  starting transfers between devices: 12.4 us -> 44.1 us
  between operations: 13.5 us -> 0.44 us
    all_gather x34 -> x0, blocking collectives: 757 us -> none  [left_blocks(): return lax.all_gather(own_piece, 'rsec', axis=1, tiled=True)]
    dot_general x34 -> x0, matrix products: 128 us -> none  [one_channel(): jnp.einsum('jit,xjtum->xjium', left_sector_tensor, right_reduced, preferr...]
    dynamic_slice x102 -> x0, local copies, waits for them, and re-layouts: 89.5 us -> none  [the longest x34 44.9 us: one_channel(): lax.dynamic_slice(enlarged_operand, (jnp.int32(0), row_start, col_start),...]
    another operation x1 -> x0, loops' own time: 44.5 us -> none  [local(): total = lax.fori_loop(0, KCH, one_channel, start_total)]
    pallas_call x0 -> x2, Pallas kernels: none -> 32.5 us  [run_channels(): pl.pallas_call(functools.partial(channels_kernel, first, count, z_first,...]
    ppermute x4 -> x25, starting transfers between devices: 12.4 us -> 44.1 us  [the longest x5 10.9 us: ring_of_four(): right = lax.ppermute(value, axis, shifted(-1))]
    unnamed x2 -> x29, local copies, waits for them, and re-layouts: 0.01 us -> 11.1 us
    ppermute x4 -> x25, waiting for transfers between devices: 33.5 us -> 41 us  [the longest x5 26.9 us: ring_of_four(): left = lax.ppermute(value, axis, shifted(1))]
  transfers between devices with their start and end apart: 5 -> 25, of which waited for: 4 -> 8; matrix products, arithmetic and copies ran while one was open for 1% -> 17% of each run, Pallas kernels for 0% -> 11%
where the time goes in v1:
time: 145 us; the launch traced here: 144 us
  starting transfers between devices  44.1 us (30%)
  waiting for transfers between devices  41 us (28%)
  Pallas kernels  32.5 us (22%)
  local copies, waits for them, and re-layouts  22.9 us (16%)
  other arithmetic  2.82 us (2%)
    pallas_call x2, Pallas kernels, run_channels(): pl.pallas_call(functools.partial(channels_kernel, first, count, z_first,...  32.5 us
    ppermute x5, waiting for transfers between devices, ring_of_four(): left = lax.ppermute(value, axis, shifted(1))  26.9 us
    unnamed x29, local copies, waits for them, and re-layouts  11.1 us
    ppermute x5, starting transfers between devices, ring_of_four(): right = lax.ppermute(value, axis, shifted(-1))  10.9 us
    ppermute x5, starting transfers between devices, ring_of_four(): far_a = lax.ppermute(left[:half], axis, shifted(1))  9.33 us
    ppermute x5, waiting for transfers between devices, ring_of_four(): far_a = lax.ppermute(left[:half], axis, shifted(1))  9.01 us
    ppermute x5, starting transfers between devices, ring_of_four(): far_b = lax.ppermute(right[half:], axis, shifted(-1))  5.67 us
    ppermute x1, starting transfers between devices, local(): lax.ppermute(jnp.concatenate([low_l[2:], own[2:], high_l[2:]], axis=1), '...  5.55 us
  transfers between devices with their start and end apart: 25, of which 8 were waited for; matrix products, arithmetic and copies ran while one was open for 17% of the time, Pallas kernels for 11%

profile of v1, /device:TPU:16, one launch (start us, length us, event | category | flops | bytes accessed | tf_op | source)
XLA Modules:
  0.0 143.8 jit_solution(16118266932360956659)
XLA Ops:
  0.0 1.3 collective-permute-start.12
  3.0 1.6 %collective-permute-start.4 = (bf16[16,4,8,128]{3,2,1,0:T(8,128)(2,1)S(1)}, bf16[16,4,8,128]{3,2,1,0:T(8,128)(2,1)S(1)}, u32[]{:S(2)}, u32[]{:S(2)}) collective-permute-start(bf16[16,4,8,128]{3,2,1,0:T(8,128)(2,1)S(1)} %get-tuple-element.15), channel_id=1, source_target_pairs={{0,4},{1,5},{2,6},{3,7},{4,8},{5,9},{6,10},{7,11},{8,12},{9,13},{1... | collective-permute-start | bytes 393224 | tf_op jit(solution)/shard_map/ppermute | solution.py:32
  4.5 1.7 %collective-permute-start.5 = (bf16[16,4,8,128]{3,2,1,0:T(8,128)(2,1)S(1)}, bf16[16,4,8,128]{3,2,1,0:T(8,128)(2,1)}, u32[]{:S(2)}, u32[]{:S(2)}) collective-permute-start(bf16[16,4,8,128]{3,2,1,0:T(8,128)(2,1)S(1)} %get-tuple-element.15), channel_id=1, source_target_pairs={{0,12},{1,13},{2,14},{3,15},{4,0},{5,1},{6,2},{7,3},{8,4},{9,5},{1... | collective-permute-start | bytes 393224 | tf_op jit(solution)/shard_map/ppermute | solution.py:33
  6.3 1.7 %fusion.4 = (bf16[18,4,8,128]{3,2,1,0:T(8,128)(2,1)}, bf16[72,4,8,128]{3,2,1,0:T(8,128)(2,1)}) fusion(bf16[34,4,8,128]{3,2,1,0:T(8,128)(2,1)} %param.7), kind=kLoop, calls=%fused_computation.25 | loop fusion | bytes 442368 | tf_op jit(solution)/shard_map/slice | solution.py:227
  8.0 1.9 %collective-permute-start.17 = (bf16[18,4,8,128]{3,2,1,0:T(8,128)(2,1)}, bf16[18,4,8,128]{3,2,1,0:T(8,128)(2,1)S(1)}, u32[]{:S(2)}, u32[]{:S(2)}) collective-permute-start(bf16[18,4,8,128]{3,2,1,0:T(8,128)(2,1)} %get-tuple-element.13), channel_id=1, source_target_pairs={{0,1},{1,2},{2,3},{3,0},{4,5},{5,6},{6,7},{7,4},{8,9},{9,10},{10,1... | collective-permute-start | bytes 442376 | tf_op jit(solution)/shard_map/ppermute | solution.py:32
  9.9 1.3 reshape.53
  13.8 2.1 %collective-permute-start.18 = (bf16[18,4,8,128]{3,2,1,0:T(8,128)(2,1)}, bf16[18,4,8,128]{3,2,1,0:T(8,128)(2,1)S(1)}, u32[]{:S(2)}, u32[]{:S(2)}) collective-permute-start(bf16[18,4,8,128]{3,2,1,0:T(8,128)(2,1)} %get-tuple-element.13), channel_id=1, source_target_pairs={{0,3},{1,0},{2,1},{3,2},{4,7},{5,4},{6,5},{7,6},{8,11},{9,8},{10,9... | collective-permute-start | bytes 442376 | tf_op jit(solution)/shard_map/ppermute | solution.py:33
  16.0 1.9 %collective-permute-start.1 = (bf16[4,2,256,128]{3,2,1,0:T(8,128)(2,1)S(1)}, bf16[4,2,256,128]{3,2,1,0:T(8,128)(2,1)S(1)}, u32[]{:S(2)}, u32[]{:S(2)}) collective-permute-start(bf16[4,2,256,128]{3,2,1,0:T(8,128)(2,1)S(1)} %get-tuple-element.7), channel_id=1, source_target_pairs={{16,0},{32,16},{48,32},{64,48},{80,64},{96,80},{112,96},{17,1},{33... | collective-permute-start | bytes 1572872 | tf_op jit(solution)/shard_map/ppermute | solution.py:216
  20.5 2.4 %collective-permute-start = (bf16[4,2,256,128]{3,2,1,0:T(8,128)(2,1)S(1)}, bf16[4,2,256,128]{3,2,1,0:T(8,128)(2,1)S(1)}, u32[]{:S(2)}, u32[]{:S(2)}) collective-permute-start(bf16[4,2,256,128]{3,2,1,0:T(8,128)(2,1)S(1)} %get-tuple-element.8), channel_id=1, source_target_pairs={{0,16},{16,32},{32,48},{48,64},{64,80},{80,96},{96,112},{1,17},{17... | collective-permute-start | bytes 1572872 | tf_op jit(solution)/shard_map/ppermute | solution.py:215
  23.9 1.4 collective-permute-start.14
  27.8 1.9 %constant_dynamic-update-slice_fusion.8 = bf16[136,4,16,128]{3,2,1,0:T(8,128)(2,1)} fusion(bf16[136,4,16,128]{3,2,1,0:T(8,128)(2,1)} %constant_dynamic-update-slice_fusion.9, bf16[34,4,16,128]{3,2,1,0:T(8,128)(2,1)} %collective-permute-done.12), kind=kLoop, calls=%fused_computation.12 | loop fusion | bytes 1114112
  29.7 1.9 %constant_dynamic-update-slice_fusion.7 = bf16[136,4,16,128]{3,2,1,0:T(8,128)(2,1)} fusion(bf16[136,4,16,128]{3,2,1,0:T(8,128)(2,1)} %constant_dynamic-update-slice_fusion.8, bf16[34,4,16,128]{3,2,1,0:T(8,128)(2,1)} %collective-permute-done.13), kind=kLoop, calls=%fused_computation.11 | loop fusion | bytes 1114112
  31.6 1.9 %collective-permute-done.14 = bf16[17,4,16,128]{3,2,1,0:T(8,128)(2,1)S(1)} collective-permute-done((bf16[17,4,16,128]{3,2,1,0:T(8,128)(2,1)S(1)}, bf16[17,4,16,128]{3,2,1,0:T(8,128)(2,1)S(1)}, u32[]{:S(2)}, u32[]{:S(2)}) %collective-permute-start.14) | collective-permute-done | bytes 278560 | tf_op jit(solution)/shard_map/ppermute | solution.py:34
  36.4 2.1 %collective-permute-start.16 = (bf16[136,4,16,128]{3,2,1,0:T(8,128)(2,1)}, bf16[136,4,16,128]{3,2,1,0:T(8,128)(2,1)}, u32[]{:S(2)}, u32[]{:S(2)}) collective-permute-start(bf16[136,4,16,128]{3,2,1,0:T(8,128)(2,1)} %constant_dynamic-update-slice_fusion.5.rights_0_), channel_id=1, source_target_pairs={{0,16},{16,0},{32,48},{48,32},{64,80},{80,64},{96,112},{112,96},{1... | collective-permute-start | bytes 6684680 | tf_op jit(solution)/shard_map/ppermute | solution.py:225
  39.2 1.6 %collective-permute-done.19 = bf16[9,4,8,128]{3,2,1,0:T(8,128)(2,1)S(1)} collective-permute-done((bf16[9,4,8,128]{3,2,1,0:T(8,128)(2,1)S(1)}, bf16[9,4,8,128]{3,2,1,0:T(8,128)(2,1)S(1)}, u32[]{:S(2)}, u32[]{:S(2)}) %collective-permute-start.19) | collective-permute-done | bytes 73760 | tf_op jit(solution)/shard_map/ppermute | solution.py:34
  40.8 1.3 collective-permute-start.20
  42.7 3.0 %collective-permute-done.20 = bf16[9,4,8,128]{3,2,1,0:T(8,128)(2,1)S(1)} collective-permute-done((bf16[9,4,8,128]{3,2,1,0:T(8,128)(2,1)S(1)}, bf16[9,4,8,128]{3,2,1,0:T(8,128)(2,1)S(1)}, u32[]{:S(2)}, u32[]{:S(2)}) %collective-permute-start.20) | collective-permute-done | bytes 73760 | tf_op jit(solution)/shard_map/ppermute | solution.py:35
  45.7 1.7 %collective-permute-start.7 = (bf16[8,4,8,128]{3,2,1,0:T(8,128)(2,1)S(1)}, bf16[8,4,8,128]{3,2,1,0:T(8,128)(2,1)S(1)}, u32[]{:S(2)}, u32[]{:S(2)}) collective-permute-start(bf16[8,4,8,128]{3,2,1,0:T(8,128)(2,1)S(1)} %slice.97), channel_id=1, source_target_pairs={{0,12},{1,13},{2,14},{3,15},{4,0},{5,1},{6,2},{7,3},{8,4},{9,5},{1... | collective-permute-start | bytes 196616 | tf_op jit(solution)/shard_map/ppermute | solution.py:35
  48.4 3.0 %collective-permute-start.22 = (bf16[72,4,8,128]{3,2,1,0:T(8,128)(2,1)}, bf16[72,4,8,128]{3,2,1,0:T(8,128)(2,1)S(1)}, u32[]{:S(2)}, u32[]{:S(2)}) collective-permute-start(bf16[72,4,8,128]{3,2,1,0:T(8,128)(2,1)} %constant_dynamic-update-slice_fusion.10.lefts_0_), channel_id=1, source_target_pairs={{0,12},{1,13},{2,14},{3,15},{4,0},{5,1},{6,2},{7,3},{8,4},{9,5},{1... | collective-permute-start | bytes 1769480 | tf_op jit(solution)/shard_map/ppermute | solution.py:33
  51.5 1.1 pad_maximum_fusion.1
  52.6 1.1 pad_maximum_fusion
  53.7 1.3 collective-permute-start.3
  55.0 5.6 %collective-permute-start.2 = (bf16[2,8,256,128]{3,2,1,0:T(8,128)(2,1)}, bf16[2,8,256,128]{3,2,1,0:T(8,128)(2,1)}, u32[]{:S(2)}, u32[]{:S(2)}) collective-permute-start(bf16[2,8,256,128]{3,2,1,0:T(8,128)(2,1)} %pad_maximum_fusion), channel_id=1, source_target_pairs={{0,1},{1,2},{2,3},{3,4},{4,5},{5,6},{6,7},{7,8},{8,9},{9,10},{10,1... | collective-permute-start | bytes 3145736 | tf_op jit(solution)/shard_map/ppermute | solution.py:217
  61.5 3.7 %collective-permute-done.21.lefts_1_ = bf16[72,4,8,128]{3,2,1,0:T(8,128)(2,1)S(1)} collective-permute-done((bf16[72,4,8,128]{3,2,1,0:T(8,128)(2,1)}, bf16[72,4,8,128]{3,2,1,0:T(8,128)(2,1)S(1)}, u32[]{:S(2)}, u32[]{:S(2)}) %collective-permute-start.21) | collective-permute-done | bytes 589856 | tf_op jit(solution)/shard_map/ppermute | solution.py:32
  65.2 3.2 %collective-permute-start.9 = (bf16[64,4,8,128]{3,2,1,0:T(8,128)(2,1)S(1)}, bf16[64,4,8,128]{3,2,1,0:T(8,128)(2,1)}, u32[]{:S(2)}, u32[]{:S(2)}) collective-permute-start(bf16[64,4,8,128]{3,2,1,0:T(8,128)(2,1)S(1)} %constant_dynamic-update-slice_fusion.lefts_0_), channel_id=1, source_target_pairs={{0,3},{1,0},{2,1},{3,2},{4,7},{5,4},{6,5},{7,6},{8,11},{9,8},{10,9... | collective-permute-start | bytes 1572872 | tf_op jit(solution)/shard_map/ppermute | solution.py:33
  69.9 23.2 %collective-permute-done.8.lefts_1_ = bf16[64,4,8,128]{3,2,1,0:T(8,128)(2,1)} collective-permute-done((bf16[64,4,8,128]{3,2,1,0:T(8,128)(2,1)S(1)}, bf16[64,4,8,128]{3,2,1,0:T(8,128)(2,1)}, u32[]{:S(2)}, u32[]{:S(2)}) %collective-permute-start.8) | collective-permute-done | bytes 524320 | tf_op jit(solution)/shard_map/ppermute | solution.py:32
  93.1 7.2 %collective-permute-start.23 = (bf16[36,4,8,128]{3,2,1,0:T(8,128)(2,1)}, bf16[36,4,8,128]{3,2,1,0:T(8,128)(2,1)}, u32[]{:S(2)}, u32[]{:S(2)}) collective-permute-start(bf16[36,4,8,128]{3,2,1,0:T(8,128)(2,1)} %slice.104), channel_id=1, source_target_pairs={{0,4},{1,5},{2,6},{3,7},{4,8},{5,9},{6,10},{7,11},{8,12},{9,13},{1... | collective-permute-start | bytes 884744 | tf_op jit(solution)/shard_map/ppermute | solution.py:34
  102.5 5.4 %collective-permute-done.23.lefts_3_ = bf16[36,4,8,128]{3,2,1,0:T(8,128)(2,1)} collective-permute-done((bf16[36,4,8,128]{3,2,1,0:T(8,128)(2,1)}, bf16[36,4,8,128]{3,2,1,0:T(8,128)(2,1)}, u32[]{:S(2)}, u32[]{:S(2)}) %collective-permute-start.23) | collective-permute-done | bytes 294944 | tf_op jit(solution)/shard_map/ppermute | solution.py:34
  107.9 1.4 collective-permute-done.24.lefts_4_
  109.3 1.8 %collective-permute-start.11 = (bf16[32,4,8,128]{3,2,1,0:T(8,128)(2,1)S(1)}, bf16[32,4,8,128]{3,2,1,0:T(8,128)(2,1)S(1)}, u32[]{:S(2)}, u32[]{:S(2)}) collective-permute-start(bf16[32,4,8,128]{3,2,1,0:T(8,128)(2,1)S(1)} %slice.99), channel_id=1, source_target_pairs={{0,3},{1,0},{2,1},{3,2},{4,7},{5,4},{6,5},{7,6},{8,11},{9,8},{10,9... | collective-permute-start | bytes 786440 | tf_op jit(solution)/shard_map/ppermute | solution.py:35
  111.2 16.5 %shard_map.64.rest_0_ = f32[4,4,128,256]{3,2,1,0:T(8,128)S(1)} custom-call(s32[34,2]{1,0:T(8,128)S(1)} %copy.9.shift, s32[4]{0:T(128)S(1)} %copy-done.4, s32[4]{0:T(128)S(1)} %copy-done.5, bf16[4,4,256,128]{3,2,1,0:T(8,128)(2,1)S(1)} %bitcast.9, bf16[4,2,256,128]{3,2,1,0:T(8,128)(2,1)S(1)} %collective-permute-done.low_l, ...), custom_call_target="tpu_custom_call" | custom-call | flops 4831838208 | bytes 10485760 | tf_op jit(solution)/shard_map/pallas_call | solution.py:191
  127.7 16.0 %shard_map.65 = bf16[2,4,128,512]{3,2,1,0:T(8,128)(2,1)} custom-call(s32[34,2]{1,0:T(8,128)S(1)} %copy.9.shift, s32[4]{0:T(128)S(1)} %copy-done.4, s32[4]{0:T(128)S(1)} %copy-done.5, bf16[4,4,256,128]{3,2,1,0:T(8,128)(2,1)S(1)} %bitcast.10, bf16[4,2,256,128]{3,2,1,0:T(8,128)(2,1)S(1)} %collective-permute-done.low_l, ...), custom_call_target="tpu_custom_call" | custom-call | flops 4294967296 | bytes 10485760 | tf_op jit(solution)/shard_map/pallas_call | solution.py:191
  (75 shorter events, 20.0 us)
Async XLA Ops:
  0.0 11.2 %copy-start.5 = (s32[4]{0:T(128)S(1)}, s32[4]{0:T(128)}, u32[]{:S(2)}) copy-start(s32[4]{0:T(128)} %right_size.3) | copy-start | bytes 52
  0.0 11.2 %copy-start.4 = (s32[4]{0:T(128)S(1)}, s32[4]{0:T(128)}, u32[]{:S(2)}) copy-start(s32[4]{0:T(128)} %left_size.3) | copy-start | bytes 52
  0.0 19.7 %collective-permute-start.12 = (bf16[34,4,16,128]{3,2,1,0:T(8,128)(2,1)}, bf16[34,4,16,128]{3,2,1,0:T(8,128)(2,1)}, u32[]{:S(2)}, u32[]{:S(2)}) collective-permute-start(bf16[34,4,16,128]{3,2,1,0:T(8,128)(2,1)} %param.8), channel_id=1, source_target_pairs={{0,32},{16,48},{32,64},{48,80},{64,96},{80,112},{96,0},{112,16},{1... | collective-permute-start | bytes 1671176 | tf_op jit(solution)/shard_map/ppermute | solution.py:32
  1.3 24.7 %collective-permute-start.13 = (bf16[34,4,16,128]{3,2,1,0:T(8,128)(2,1)}, bf16[34,4,16,128]{3,2,1,0:T(8,128)(2,1)}, u32[]{:S(2)}, u32[]{:S(2)}) collective-permute-start(bf16[34,4,16,128]{3,2,1,0:T(8,128)(2,1)} %param.8), channel_id=1, source_target_pairs={{0,96},{16,112},{32,0},{48,16},{64,32},{80,48},{96,64},{112,80},{1... | collective-permute-start | bytes 1671176 | tf_op jit(solution)/shard_map/ppermute | solution.py:33
  3.0 10.9 %collective-permute-start.4 = (bf16[16,4,8,128]{3,2,1,0:T(8,128)(2,1)S(1)}, bf16[16,4,8,128]{3,2,1,0:T(8,128)(2,1)S(1)}, u32[]{:S(2)}, u32[]{:S(2)}) collective-permute-start(bf16[16,4,8,128]{3,2,1,0:T(8,128)(2,1)S(1)} %get-tuple-element.15), channel_id=1, source_target_pairs={{0,4},{1,5},{2,6},{3,7},{4,8},{5,9},{6,10},{7,11},{8,12},{9,13},{1... | collective-permute-start | bytes 393224 | tf_op jit(solution)/shard_map/ppermute | solution.py:32
  4.5 11.4 %collective-permute-start.5 = (bf16[16,4,8,128]{3,2,1,0:T(8,128)(2,1)S(1)}, bf16[16,4,8,128]{3,2,1,0:T(8,128)(2,1)}, u32[]{:S(2)}, u32[]{:S(2)}) collective-permute-start(bf16[16,4,8,128]{3,2,1,0:T(8,128)(2,1)S(1)} %get-tuple-element.15), channel_id=1, source_target_pairs={{0,12},{1,13},{2,14},{3,15},{4,0},{5,1},{6,2},{7,3},{8,4},{9,5},{1... | collective-permute-start | bytes 393224 | tf_op jit(solution)/shard_map/ppermute | solution.py:33
  8.0 16.0 %collective-permute-start.17 = (bf16[18,4,8,128]{3,2,1,0:T(8,128)(2,1)}, bf16[18,4,8,128]{3,2,1,0:T(8,128)(2,1)S(1)}, u32[]{:S(2)}, u32[]{:S(2)}) collective-permute-start(bf16[18,4,8,128]{3,2,1,0:T(8,128)(2,1)} %get-tuple-element.13), channel_id=1, source_target_pairs={{0,1},{1,2},{2,3},{3,0},{4,5},{5,6},{6,7},{7,4},{8,9},{9,10},{10,1... | collective-permute-start | bytes 442376 | tf_op jit(solution)/shard_map/ppermute | solution.py:32
  13.8 2.1 %copy-start.7 = (bf16[16,4,8,128]{3,2,1,0:T(8,128)(2,1)}, bf16[16,4,8,128]{3,2,1,0:T(8,128)(2,1)S(1)}, u32[]{:S(2)}) copy-start(bf16[16,4,8,128]{3,2,1,0:T(8,128)(2,1)S(1)} %collective-permute-done.4) | copy-start | bytes 393220
  13.8 22.6 %collective-permute-start.18 = (bf16[18,4,8,128]{3,2,1,0:T(8,128)(2,1)}, bf16[18,4,8,128]{3,2,1,0:T(8,128)(2,1)S(1)}, u32[]{:S(2)}, u32[]{:S(2)}) collective-permute-start(bf16[18,4,8,128]{3,2,1,0:T(8,128)(2,1)} %get-tuple-element.13), channel_id=1, source_target_pairs={{0,3},{1,0},{2,1},{3,2},{4,7},{5,4},{6,5},{7,6},{8,11},{9,8},{10,9... | collective-permute-start | bytes 442376 | tf_op jit(solution)/shard_map/ppermute | solution.py:33
  16.0 32.1 %collective-permute-start.1 = (bf16[4,2,256,128]{3,2,1,0:T(8,128)(2,1)S(1)}, bf16[4,2,256,128]{3,2,1,0:T(8,128)(2,1)S(1)}, u32[]{:S(2)}, u32[]{:S(2)}) collective-permute-start(bf16[4,2,256,128]{3,2,1,0:T(8,128)(2,1)S(1)} %get-tuple-element.7), channel_id=1, source_target_pairs={{16,0},{32,16},{48,32},{64,48},{80,64},{96,80},{112,96},{17,1},{33... | collective-permute-start | bytes 1572872 | tf_op jit(solution)/shard_map/ppermute | solution.py:216
  20.5 27.9 %collective-permute-start = (bf16[4,2,256,128]{3,2,1,0:T(8,128)(2,1)S(1)}, bf16[4,2,256,128]{3,2,1,0:T(8,128)(2,1)S(1)}, u32[]{:S(2)}, u32[]{:S(2)}) collective-permute-start(bf16[4,2,256,128]{3,2,1,0:T(8,128)(2,1)S(1)} %get-tuple-element.8), channel_id=1, source_target_pairs={{0,16},{16,32},{32,48},{48,64},{64,80},{80,96},{96,112},{1,17},{17... | collective-permute-start | bytes 1572872 | tf_op jit(solution)/shard_map/ppermute | solution.py:215
  23.9 9.6 %collective-permute-start.14 = (bf16[17,4,16,128]{3,2,1,0:T(8,128)(2,1)S(1)}, bf16[17,4,16,128]{3,2,1,0:T(8,128)(2,1)S(1)}, u32[]{:S(2)}, u32[]{:S(2)}) collective-permute-start(bf16[17,4,16,128]{3,2,1,0:T(8,128)(2,1)S(1)} %slice.100), channel_id=1, source_target_pairs={{0,32},{16,48},{32,64},{48,80},{64,96},{80,112},{96,0},{112,16},{1... | collective-permute-start | bytes 835592 | tf_op jit(solution)/shard_map/ppermute | solution.py:34
  27.0 8.2 %collective-permute-start.15 = (bf16[17,4,16,128]{3,2,1,0:T(8,128)(2,1)S(1)}, bf16[17,4,16,128]{3,2,1,0:T(8,128)(2,1)S(1)}, u32[]{:S(2)}, u32[]{:S(2)}) collective-permute-start(bf16[17,4,16,128]{3,2,1,0:T(8,128)(2,1)S(1)} %slice.101), channel_id=1, source_target_pairs={{0,96},{16,112},{32,0},{48,16},{64,32},{80,48},{96,64},{112,80},{1... | collective-permute-start | bytes 835592 | tf_op jit(solution)/shard_map/ppermute | solution.py:35
  33.5 20.1 %collective-permute-start.6 = (bf16[8,4,8,128]{3,2,1,0:T(8,128)(2,1)S(1)}, bf16[8,4,8,128]{3,2,1,0:T(8,128)(2,1)S(1)}, u32[]{:S(2)}, u32[]{:S(2)}) collective-permute-start(bf16[8,4,8,128]{3,2,1,0:T(8,128)(2,1)S(1)} %slice.96), channel_id=1, source_target_pairs={{0,4},{1,5},{2,6},{3,7},{4,8},{5,9},{6,10},{7,11},{8,12},{9,13},{1... | collective-permute-start | bytes 196616 | tf_op jit(solution)/shard_map/ppermute | solution.py:34
  35.2 5.6 %collective-permute-start.19 = (bf16[9,4,8,128]{3,2,1,0:T(8,128)(2,1)S(1)}, bf16[9,4,8,128]{3,2,1,0:T(8,128)(2,1)S(1)}, u32[]{:S(2)}, u32[]{:S(2)}) collective-permute-start(bf16[9,4,8,128]{3,2,1,0:T(8,128)(2,1)S(1)} %slice.102), channel_id=1, source_target_pairs={{0,1},{1,2},{2,3},{3,0},{4,5},{5,6},{6,7},{7,4},{8,9},{9,10},{10,1... | collective-permute-start | bytes 221192 | tf_op jit(solution)/shard_map/ppermute | solution.py:34
  36.4 74.8 %collective-permute-start.16 = (bf16[136,4,16,128]{3,2,1,0:T(8,128)(2,1)}, bf16[136,4,16,128]{3,2,1,0:T(8,128)(2,1)}, u32[]{:S(2)}, u32[]{:S(2)}) collective-permute-start(bf16[136,4,16,128]{3,2,1,0:T(8,128)(2,1)} %constant_dynamic-update-slice_fusion.5.rights_0_), channel_id=1, source_target_pairs={{0,16},{16,0},{32,48},{48,32},{64,80},{80,64},{96,112},{112,96},{1... | collective-permute-start | bytes 6684680 | tf_op jit(solution)/shard_map/ppermute | solution.py:225
  40.8 4.9 %collective-permute-start.20 = (bf16[9,4,8,128]{3,2,1,0:T(8,128)(2,1)S(1)}, bf16[9,4,8,128]{3,2,1,0:T(8,128)(2,1)S(1)}, u32[]{:S(2)}, u32[]{:S(2)}) collective-permute-start(bf16[9,4,8,128]{3,2,1,0:T(8,128)(2,1)S(1)} %slice.103), channel_id=1, source_target_pairs={{0,3},{1,0},{2,1},{3,2},{4,7},{5,4},{6,5},{7,6},{8,11},{9,8},{10,9... | collective-permute-start | bytes 221192 | tf_op jit(solution)/shard_map/ppermute | solution.py:35
  45.7 9.3 %collective-permute-start.7 = (bf16[8,4,8,128]{3,2,1,0:T(8,128)(2,1)S(1)}, bf16[8,4,8,128]{3,2,1,0:T(8,128)(2,1)S(1)}, u32[]{:S(2)}, u32[]{:S(2)}) collective-permute-start(bf16[8,4,8,128]{3,2,1,0:T(8,128)(2,1)S(1)} %slice.97), channel_id=1, source_target_pairs={{0,12},{1,13},{2,14},{3,15},{4,0},{5,1},{6,2},{7,3},{8,4},{9,5},{1... | collective-permute-start | bytes 196616 | tf_op jit(solution)/shard_map/ppermute | solution.py:35
  48.1 17.1 %collective-permute-start.21 = (bf16[72,4,8,128]{3,2,1,0:T(8,128)(2,1)}, bf16[72,4,8,128]{3,2,1,0:T(8,128)(2,1)S(1)}, u32[]{:S(2)}, u32[]{:S(2)}) collective-permute-start(bf16[72,4,8,128]{3,2,1,0:T(8,128)(2,1)} %constant_dynamic-update-slice_fusion.10.lefts_0_), channel_id=1, source_target_pairs={{0,4},{1,5},{2,6},{3,7},{4,8},{5,9},{6,10},{7,11},{8,12},{9,13},{1... | collective-permute-start | bytes 1769480 | tf_op jit(solution)/shard_map/ppermute | solution.py:32
  48.4 16.7 %collective-permute-start.22 = (bf16[72,4,8,128]{3,2,1,0:T(8,128)(2,1)}, bf16[72,4,8,128]{3,2,1,0:T(8,128)(2,1)S(1)}, u32[]{:S(2)}, u32[]{:S(2)}) collective-permute-start(bf16[72,4,8,128]{3,2,1,0:T(8,128)(2,1)} %constant_dynamic-update-slice_fusion.10.lefts_0_), channel_id=1, source_target_pairs={{0,12},{1,13},{2,14},{3,15},{4,0},{5,1},{6,2},{7,3},{8,4},{9,5},{1... | collective-permute-start | bytes 1769480 | tf_op jit(solution)/shard_map/ppermute | solution.py:33
  51.5 9.1 %copy-start.1 = (bf16[64,4,8,128]{3,2,1,0:T(8,128)(2,1)S(1)}, bf16[64,4,8,128]{3,2,1,0:T(8,128)(2,1)}, u32[]{:S(2)}) copy-start(bf16[64,4,8,128]{3,2,1,0:T(8,128)(2,1)} %copy-done) | copy-start | bytes 1572868
  52.6 47.9 %copy-start.8 = (s32[34,2]{0,1:T(2,128)S(1)}, s32[34,2]{0,1:T(2,128)}, u32[]{:S(2)}) copy-start(s32[34,2]{0,1:T(2,128)} %param.11) | copy-start | bytes 820
  53.7 57.5 %collective-permute-start.3 = (bf16[2,8,256,128]{3,2,1,0:T(8,128)(2,1)}, bf16[2,8,256,128]{3,2,1,0:T(8,128)(2,1)}, u32[]{:S(2)}, u32[]{:S(2)}) collective-permute-start(bf16[2,8,256,128]{3,2,1,0:T(8,128)(2,1)} %pad_maximum_fusion.1), channel_id=1, source_target_pairs={{1,0},{2,1},{3,2},{4,3},{5,4},{6,5},{7,6},{8,7},{9,8},{10,9},{11,1... | collective-permute-start | bytes 3145736 | tf_op jit(solution)/shard_map/ppermute | solution.py:220
  55.0 56.2 %collective-permute-start.2 = (bf16[2,8,256,128]{3,2,1,0:T(8,128)(2,1)}, bf16[2,8,256,128]{3,2,1,0:T(8,128)(2,1)}, u32[]{:S(2)}, u32[]{:S(2)}) collective-permute-start(bf16[2,8,256,128]{3,2,1,0:T(8,128)(2,1)} %pad_maximum_fusion), channel_id=1, source_target_pairs={{0,1},{1,2},{2,3},{3,4},{4,5},{5,6},{6,7},{7,8},{8,9},{9,10},{10,1... | collective-permute-start | bytes 3145736 | tf_op jit(solution)/shard_map/ppermute | solution.py:217
  61.5 3.7 %copy-start.2 = (bf16[64,4,8,128]{3,2,1,0:T(8,128)(2,1)}, bf16[64,4,8,128]{3,2,1,0:T(8,128)(2,1)S(1)}, u32[]{:S(2)}) copy-start(bf16[64,4,8,128]{3,2,1,0:T(8,128)(2,1)S(1)} %constant_dynamic-update-slice_fusion.lefts_0_) | copy-start | bytes 1572868
  65.2 28.0 %collective-permute-start.8 = (bf16[64,4,8,128]{3,2,1,0:T(8,128)(2,1)S(1)}, bf16[64,4,8,128]{3,2,1,0:T(8,128)(2,1)}, u32[]{:S(2)}, u32[]{:S(2)}) collective-permute-start(bf16[64,4,8,128]{3,2,1,0:T(8,128)(2,1)S(1)} %constant_dynamic-update-slice_fusion.lefts_0_), channel_id=1, source_target_pairs={{0,1},{1,2},{2,3},{3,0},{4,5},{5,6},{6,7},{7,4},{8,9},{9,10},{10,1... | collective-permute-start | bytes 1572872 | tf_op jit(solution)/shard_map/ppermute | solution.py:32
  65.2 35.2 %collective-permute-start.9 = (bf16[64,4,8,128]{3,2,1,0:T(8,128)(2,1)S(1)}, bf16[64,4,8,128]{3,2,1,0:T(8,128)(2,1)}, u32[]{:S(2)}, u32[]{:S(2)}) collective-permute-start(bf16[64,4,8,128]{3,2,1,0:T(8,128)(2,1)S(1)} %constant_dynamic-update-slice_fusion.lefts_0_), channel_id=1, source_target_pairs={{0,3},{1,0},{2,1},{3,2},{4,7},{5,4},{6,5},{7,6},{8,11},{9,8},{10,9... | collective-permute-start | bytes 1572872 | tf_op jit(solution)/shard_map/ppermute | solution.py:33
  93.1 14.8 %collective-permute-start.23 = (bf16[36,4,8,128]{3,2,1,0:T(8,128)(2,1)}, bf16[36,4,8,128]{3,2,1,0:T(8,128)(2,1)}, u32[]{:S(2)}, u32[]{:S(2)}) collective-permute-start(bf16[36,4,8,128]{3,2,1,0:T(8,128)(2,1)} %slice.104), channel_id=1, source_target_pairs={{0,4},{1,5},{2,6},{3,7},{4,8},{5,9},{6,10},{7,11},{8,12},{9,13},{1... | collective-permute-start | bytes 884744 | tf_op jit(solution)/shard_map/ppermute | solution.py:34
  100.4 9.0 %collective-permute-start.24 = (bf16[36,4,8,128]{3,2,1,0:T(8,128)(2,1)}, bf16[36,4,8,128]{3,2,1,0:T(8,128)(2,1)}, u32[]{:S(2)}, u32[]{:S(2)}) collective-permute-start(bf16[36,4,8,128]{3,2,1,0:T(8,128)(2,1)} %slice.105), channel_id=1, source_target_pairs={{0,12},{1,13},{2,14},{3,15},{4,0},{5,1},{6,2},{7,3},{8,4},{9,5},{1... | collective-permute-start | bytes 884744 | tf_op jit(solution)/shard_map/ppermute | solution.py:35
  102.5 25.2 %copy-start.3 = (bf16[64,4,8,128]{3,2,1,0:T(8,128)(2,1)S(1)}, bf16[64,4,8,128]{3,2,1,0:T(8,128)(2,1)}, u32[]{:S(2)}) copy-start(bf16[64,4,8,128]{3,2,1,0:T(8,128)(2,1)} %copy-done.2) | copy-start | bytes 1572868
  107.9 19.7 %collective-permute-start.10 = (bf16[32,4,8,128]{3,2,1,0:T(8,128)(2,1)S(1)}, bf16[32,4,8,128]{3,2,1,0:T(8,128)(2,1)S(1)}, u32[]{:S(2)}, u32[]{:S(2)}) collective-permute-start(bf16[32,4,8,128]{3,2,1,0:T(8,128)(2,1)S(1)} %slice.98), channel_id=1, source_target_pairs={{0,1},{1,2},{2,3},{3,0},{4,5},{5,6},{6,7},{7,4},{8,9},{9,10},{10,1... | collective-permute-start | bytes 786440 | tf_op jit(solution)/shard_map/ppermute | solution.py:34
  109.3 18.3 %collective-permute-start.11 = (bf16[32,4,8,128]{3,2,1,0:T(8,128)(2,1)S(1)}, bf16[32,4,8,128]{3,2,1,0:T(8,128)(2,1)S(1)}, u32[]{:S(2)}, u32[]{:S(2)}) collective-permute-start(bf16[32,4,8,128]{3,2,1,0:T(8,128)(2,1)S(1)} %slice.99), channel_id=1, source_target_pairs={{0,3},{1,0},{2,1},{3,2},{4,7},{5,4},{6,5},{7,6},{8,11},{9,8},{10,9... | collective-permute-start | bytes 786440 | tf_op jit(solution)/shard_map/ppermute | solution.py:35
  (2 other events, 1.9 us)

commit v2 on v1

v2 whole, which is shorter than its diff:
```python
import functools

import jax
import jax.numpy as jnp
from jax import lax
from jax.experimental import pallas as pl
from jax.experimental.pallas import tpu as pltpu
from jax.sharding import PartitionSpec as P

KCH = 34
SHIFT = 2
SPLIT = 16
XN, ZN, YN, CORES = 4, 4, 4, 2
NT = (((1,), (1,)), ((), ()))
NN = (((1,), (0,)), ((), ()))


def shifted_x(step):
    return [(ZN * x + z, ZN * ((x + step) % XN) + z) for x in range(XN) for z in range(ZN)]


def shifted_z(step):
    return [(ZN * x + z, ZN * x + (z + step) % ZN) for x in range(XN) for z in range(ZN)]


def shifted_y(step):
    return [(CORES * y + c, CORES * ((y + step) % YN) + c) for y in range(YN) for c in range(CORES)]


def mask_kernel(left_size, right_size, two_site, down, up):
    row = lax.broadcasted_iota(jnp.int32, (128, 128), 0)
    col = lax.broadcasted_iota(jnp.int32, (128, 128), 1)
    for l in range(4):
        for r in range(4):
            live = (row < left_size[l]) & (col < right_size[r])
            target = down if r < 2 else up
            for v in range(2):
                block = two_site[v, l, :, r * 128 : r * 128 + 128].astype(jnp.float32)
                target[r % 2, l, v * 128 : v * 128 + 128] = jnp.where(live, block, 0.0).astype(
                    jnp.bfloat16
                )


def masked_halves(two_site, left_size, right_size):
    half = jax.ShapeDtypeStruct((2, 4, 256, 128), jnp.bfloat16)
    smem = pl.BlockSpec(memory_space=pltpu.SMEM)
    vmem = pl.BlockSpec(memory_space=pltpu.VMEM)
    return pl.pallas_call(
        mask_kernel,
        out_shape=(half, half),
        in_specs=[smem, smem, vmem],
        out_specs=(vmem, vmem),
        compiler_params=pltpu.CompilerParams(vmem_limit_bytes=8 << 20),
        cost_estimate=pl.CostEstimate(flops=1 << 20, bytes_accessed=2 << 20, transcendentals=0),
    )(left_size, right_size, two_site)


def rim_kernel(low_r, down, up, high_r, to_next, to_previous):
    for at, part in enumerate((low_r, down, up, high_r)):
        to_next[2 * at : 2 * at + 2] = part[:, 2:4]
        to_previous[2 * at : 2 * at + 2] = part[:, 0:2]


def left_rims(low_r, down, up, high_r):
    rim = jax.ShapeDtypeStruct((8, 2, 256, 128), jnp.bfloat16)
    vmem = pl.BlockSpec(memory_space=pltpu.VMEM)
    return pl.pallas_call(
        rim_kernel,
        out_shape=(rim, rim),
        in_specs=[vmem] * 4,
        out_specs=(vmem, vmem),
        compiler_params=pltpu.CompilerParams(vmem_limit_bytes=12 << 20),
        cost_estimate=pl.CostEstimate(flops=1 << 20, bytes_accessed=4 << 20, transcendentals=0),
    )(low_r, down, up, high_r)


def bundle_kernel(own, left, right, far, first, second):
    for at, part in enumerate((own, left, right, far)):
        first[at] = part[:SPLIT]
        second[at] = part[SPLIT:]


def bundled(own, left, right, far):
    vmem = pl.BlockSpec(memory_space=pltpu.VMEM)
    return pl.pallas_call(
        bundle_kernel,
        out_shape=tuple(
            jax.ShapeDtypeStruct((4, many, 4, 8, 128), jnp.bfloat16)
            for many in (SPLIT, KCH - SPLIT)
        ),
        in_specs=[vmem] * 4,
        out_specs=(vmem, vmem),
        compiler_params=pltpu.CompilerParams(vmem_limit_bytes=8 << 20),
        cost_estimate=pl.CostEstimate(flops=1 << 20, bytes_accessed=2 << 20, transcendentals=0),
    )(own, left, right, far)


RING_STEPS = (0, -1, 1, 2)


def channels_kernel(
    first, count, is_first, is_last, shift, left_size, right_size,
    low_r, down, up, high_r, low_l, high_l, lefts, rights, partners, *rest,
):
    rest = list(rest)
    total_in = None if is_first else rest.pop(0)
    out = rest.pop(0)
    source, left_all, right_all = rest[:3]
    rest = rest[3:]
    total = rest.pop(0) if is_last else out
    sems = rest.pop(0)
    rsec, lsec = lax.axis_index("rsec"), lax.axis_index("lsec")
    x, z, y, core = rsec // ZN, lax.rem(rsec, ZN), lsec // CORES, lax.rem(lsec, CORES)

    copies = []

    def start(src, dst):
        copy = pltpu.make_async_copy(src, dst, sems.at[len(copies)])
        copy.start()
        copies.append(copy)

    for at, part in enumerate((low_r, down, up, high_r)):
        start(part, source.at[2 * at : 2 * at + 2, 2:6])
    start(low_l, source.at[:, 0:2])
    start(high_l, source.at[:, 6:8])
    for step, own, other in zip(RING_STEPS, rights, partners):
        for part, side in ((own, core), (other, 1 - core)):
            row = pl.multiple_of(16 * (CORES * lax.rem(y + step + YN, YN) + side), 16)
            start(part.at[first : first + count], right_all.at[:, :, pl.ds(row, 16)])
    for dx, bundle in zip(RING_STEPS, lefts):
        for at, dz in enumerate(RING_STEPS):
            row = 8 * (ZN * lax.rem(x + dx + XN, XN) + lax.rem(z + dz + ZN, ZN))
            start(bundle.at[at], left_all.at[:, :, pl.ds(pl.multiple_of(row, 8), 8)])
    if is_first:
        total[...] = jnp.zeros_like(total)
    else:
        start(total_in, total)
    for copy in copies:
        copy.wait()

    def two_channels(pair, carry):
        ks = (2 * pair, 2 * pair + 1)
        shifts = [(shift[first + k, 0], shift[first + k, 1]) for k in ks]
        for r in range(4):
            partial = []
            for k, (dl, dr) in zip(ks, shifts):
                rows = source[r + SHIFT - dr, pl.ds(SHIFT - dl, 4)].reshape(4 * 256, 128)
                partial.append(
                    lax.dot_general(
                        rows, right_all[k, r], NT, preferred_element_type=jnp.float32
                    ).astype(jnp.bfloat16)
                )
            for l in range(4):
                stacked = jnp.concatenate(
                    [
                        jnp.concatenate(
                            [p[l * 256 : l * 256 + 128], p[l * 256 + 128 : l * 256 + 256]], axis=1
                        )
                        for p in partial
                    ],
                    axis=0,
                )
                sides = jnp.concatenate([left_all[k, l] for k in ks], axis=1)
                total[l, r] += lax.dot_general(
                    sides, stacked, NN, preferred_element_type=jnp.float32
                )
        return carry

    lax.fori_loop(0, count // 2, two_channels, 0)

    if is_last:
        row = lax.broadcasted_iota(jnp.int32, (128, 128), 0)
        col = lax.broadcasted_iota(jnp.int32, (128, 128), 1)
        for l in range(4):
            for r in range(4):
                live = (row < left_size[l]) & (col < right_size[r])
                for v in range(2):
                    block = total[l, r, :, v * 128 : v * 128 + 128]
                    out[v, l, :, r * 128 : r * 128 + 128] = jnp.where(live, block, 0.0).astype(
                        jnp.bfloat16
                    )


def run_channels(first, count, is_first, is_last, scalars, sources, lefts, rights, partners, total):
    totals = jax.ShapeDtypeStruct((4, 4, 128, 256), jnp.float32)
    result = jax.ShapeDtypeStruct((2, 4, 128, 512), jnp.bfloat16)
    anywhere = pl.BlockSpec(memory_space=pltpu.HBM)
    smem = pl.BlockSpec(memory_space=pltpu.SMEM)
    operands = [*scalars, *sources, tuple(lefts), tuple(rights), tuple(partners)]
    specs = [smem] * 3 + [anywhere] * 6 + [(anywhere,) * 4] * 3
    if not is_first:
        operands.append(total)
        specs.append(anywhere)
    scratch = [
        pltpu.VMEM((8, 8, 256, 128), jnp.bfloat16),
        pltpu.VMEM((count, 4, 128, 128), jnp.bfloat16),
        pltpu.VMEM((count, 4, 128, 128), jnp.bfloat16),
    ]
    if is_last:
        scratch.append(pltpu.VMEM((4, 4, 128, 256), jnp.float32))
    scratch.append(pltpu.SemaphoreType.DMA((40,)))
    return pl.pallas_call(
        functools.partial(channels_kernel, first, count, is_first, is_last),
        out_shape=result if is_last else totals,
        in_specs=specs,
        out_specs=pl.BlockSpec(memory_space=pltpu.VMEM),
        scratch_shapes=scratch,
        compiler_params=pltpu.CompilerParams(vmem_limit_bytes=60 * 1024 * 1024),
        cost_estimate=pl.CostEstimate(
            flops=count * 4 * 4 * 2 * 2 * 2 * 128**3, bytes_accessed=10 << 20, transcendentals=0
        ),
    )(*operands)


def local(two_site, left_env, right_env, left_size, right_size, channel_shift):
    down, up = masked_halves(two_site, left_size, right_size)
    l_up = [(i, i + 1) for i in range(7)]
    l_down = [(i + 1, i) for i in range(7)]
    r_up = [(i, i + 1) for i in range(15)]
    r_down = [(i + 1, i) for i in range(15)]
    low_r = lax.ppermute(up, "rsec", r_up)
    high_r = lax.ppermute(down, "rsec", r_down)
    to_next, to_previous = left_rims(low_r, down, up, high_r)
    low_l = lax.ppermute(to_next, "lsec", l_up)
    high_l = lax.ppermute(to_previous, "lsec", l_down)

    z_ring = [lax.ppermute(left_env, "rsec", shifted_z(step)) for step in (1, -1, 2)]
    rights = [right_env] + [lax.ppermute(right_env, "lsec", shifted_y(s)) for s in (1, -1, 2)]
    swap = [(i, i ^ 1) for i in range(8)]
    partners = [lax.ppermute(part, "lsec", swap) for part in rights]

    bundle_a, bundle_b = bundled(left_env, *z_ring)
    left_a = lax.ppermute(bundle_a, "rsec", shifted_x(1))
    right_a = lax.ppermute(bundle_a, "rsec", shifted_x(-1))
    far_a = lax.ppermute(left_a, "rsec", shifted_x(1))
    left_b = lax.ppermute(bundle_b, "rsec", shifted_x(1))
    right_b = lax.ppermute(bundle_b, "rsec", shifted_x(-1))
    far_b = lax.ppermute(right_b, "rsec", shifted_x(-1))

    scalars = (channel_shift, left_size, right_size)
    sources = (low_r, down, up, high_r, low_l, high_l)
    lefts_a = (bundle_a, left_a, right_a, far_a)
    lefts_b = (bundle_b, left_b, right_b, far_b)
    total = run_channels(
        0, SPLIT, True, False, scalars, sources, lefts_a, rights, partners, None
    )
    return run_channels(
        SPLIT, KCH - SPLIT, False, True, scalars, sources, lefts_b, rights, partners, total
    )


def solution(mesh):
    placed = (
        P(None, "lsec", None, "rsec"),
        P(None, "lsec", "rsec", None),
        P(None, "rsec", "lsec", None),
        P("lsec"),
        P("rsec"),
        P(),
    )
    return jax.shard_map(
        local, mesh=mesh, in_specs=placed, out_specs=P(None, "lsec", None, "rsec"), check_vma=False
    )
```

time: 145 us -> 122 us (0.84)
  local copies, waits for them, and re-layouts: 22.9 us -> 5.26 us
  starting transfers between devices: 44.1 us -> 32.6 us
  Pallas kernels: 32.5 us -> 38.7 us
  waiting for transfers between devices: 41 us -> 43.9 us
  other arithmetic: 2.82 us -> 0 us
    ppermute x25 -> x20, starting transfers between devices: 44.1 us -> 32.6 us  [the longest x3 6.78 us: local(): lax.ppermute(left_env, 'rsec', shifted_z(step))]
    slice x16 -> x0, local copies, waits for them, and re-layouts: 9.09 us -> none  [the longest x5 3.53 us: ring_of_four(): far_b = lax.ppermute(right[half:], axis, shifted(-1))]
    pallas_call x2 -> x5, Pallas kernels: 32.5 us -> 38.7 us  [the longest x2 35.7 us: run_channels(): pl.pallas_call(functools.partial(channels_kernel, first, count, is_first,...]
    unnamed x29 -> x37, local copies, waits for them, and re-layouts: 11.1 us -> 5.26 us
    ppermute x25 -> x20, waiting for transfers between devices: 41 us -> 43.9 us  [the longest x3 17.8 us: local(): lax.ppermute(left_env, 'rsec', shifted_z(step))]
    concatenate x2 -> x0, other arithmetic: 2.18 us -> none  [the longest x1 1.09 us: local(): jnp.concatenate([low_l[:2], own[:2], high_l[:2]], axis=1)]
  transfers between devices with their start and end apart: 25 -> 20, of which waited for: 8 -> 6; matrix products, arithmetic and copies ran while one was open for 17% -> 1% of each run, Pallas kernels for 11% -> 16%
where the time goes in v2:
time: 122 us; the launch traced here: 121 us
  waiting for transfers between devices  43.9 us (36%)
  Pallas kernels  38.7 us (32%)
  starting transfers between devices  32.6 us (27%)
  local copies, waits for them, and re-layouts  5.26 us (4%)
    pallas_call x2, Pallas kernels, run_channels(): pl.pallas_call(functools.partial(channels_kernel, first, count, is_first,...  35.7 us
    ppermute x3, waiting for transfers between devices, local(): lax.ppermute(left_env, 'rsec', shifted_z(step))  17.8 us
    ppermute x1, waiting for transfers between devices, local(): far_a = lax.ppermute(left_a, 'rsec', shifted_x(1))  9.63 us
    ppermute x1, waiting for transfers between devices, local(): right_a = lax.ppermute(bundle_a, 'rsec', shifted_x(-1))  7.74 us
    ppermute x3, starting transfers between devices, local(): lax.ppermute(left_env, 'rsec', shifted_z(step))  6.78 us
    unnamed x37, local copies, waits for them, and re-layouts  5.26 us
    ppermute x1, starting transfers between devices, local(): high_l = lax.ppermute(to_previous, 'lsec', l_down)  4.99 us
    ppermute x3, waiting for transfers between devices, local(): lax.ppermute(right_env, 'lsec', shifted_y(s))  4.71 us
  transfers between devices with their start and end apart: 20, of which 6 were waited for; matrix products, arithmetic and copies ran while one was open for 1% of the time, Pallas kernels for 16%

profile of v2, /device:TPU:16, one launch (start us, length us, event | category | flops | bytes accessed | tf_op | source)
XLA Modules:
  0.0 120.7 jit_solution(11796286530869463747)
XLA Ops:
  0.0 1.9 %collective-permute-start.4 = (bf16[34,4,8,128]{3,2,1,0:T(8,128)(2,1)}, bf16[34,4,8,128]{3,2,1,0:T(8,128)(2,1)S(1)}, u32[]{:S(2)}, u32[]{:S(2)}) collective-permute-start(bf16[34,4,8,128]{3,2,1,0:T(8,128)(2,1)} %own.1), channel_id=1, source_target_pairs={{0,1},{1,2},{2,3},{3,0},{4,5},{5,6},{6,7},{7,4},{8,9},{9,10},{10,1... | collective-permute-start | bytes 835592 | tf_op jit(solution)/shard_map/ppermute | solution.py:227
  1.9 1.2 %copy-done = bf16[2,4,128,512]{3,2,1,0:T(8,128)(2,1)S(1)} copy-done((bf16[2,4,128,512]{3,2,1,0:T(8,128)(2,1)S(1)}, bf16[2,4,128,512]{3,2,1,0:T(8,128)(2,1)}, u32[]{:S(2)}) %copy-start) | copy-done | bytes 1048600
  3.1 0.7 copy-done.6
  3.8 0.7 copy-done.7
  4.5 0.8 shard_map.64
  5.3 3.9 %collective-permute-start = (bf16[2,4,256,128]{3,2,1,0:T(8,128)(2,1)S(1)}, bf16[2,4,256,128]{3,2,1,0:T(8,128)(2,1)S(1)}, u32[]{:S(2)}, u32[]{:S(2)}) collective-permute-start(bf16[2,4,256,128]{3,2,1,0:T(8,128)(2,1)S(1)} %get-tuple-element.11.up), channel_id=1, source_target_pairs={{0,1},{1,2},{2,3},{3,4},{4,5},{5,6},{6,7},{7,8},{8,9},{9,10},{10,1... | collective-permute-start | bytes 1572872 | tf_op jit(solution)/shard_map/ppermute | solution.py:221
  9.2 2.3 %collective-permute-start.5 = (bf16[34,4,8,128]{3,2,1,0:T(8,128)(2,1)}, bf16[34,4,8,128]{3,2,1,0:T(8,128)(2,1)S(1)}, u32[]{:S(2)}, u32[]{:S(2)}) collective-permute-start(bf16[34,4,8,128]{3,2,1,0:T(8,128)(2,1)} %own.1), channel_id=1, source_target_pairs={{0,3},{1,0},{2,1},{3,2},{4,7},{5,4},{6,5},{7,6},{8,11},{9,8},{10,9... | collective-permute-start | bytes 835592 | tf_op jit(solution)/shard_map/ppermute | solution.py:227
  11.4 1.3 %collective-permute-start.1 = (bf16[2,4,256,128]{3,2,1,0:T(8,128)(2,1)S(1)}, bf16[2,4,256,128]{3,2,1,0:T(8,128)(2,1)S(1)}, u32[]{:S(2)}, u32[]{:S(2)}) collective-permute-start(bf16[2,4,256,128]{3,2,1,0:T(8,128)(2,1)S(1)} %get-tuple-element.12.down), channel_id=1, source_target_pairs={{1,0},{2,1},{3,2},{4,3},{5,4},{6,5},{7,6},{8,7},{9,8},{10,9},{11,1... | collective-permute-start | bytes 1572872 | tf_op jit(solution)/shard_map/ppermute | solution.py:222
  12.7 2.6 %collective-permute-start.6 = (bf16[34,4,8,128]{3,2,1,0:T(8,128)(2,1)}, bf16[34,4,8,128]{3,2,1,0:T(8,128)(2,1)S(1)}, u32[]{:S(2)}, u32[]{:S(2)}) collective-permute-start(bf16[34,4,8,128]{3,2,1,0:T(8,128)(2,1)} %own.1), channel_id=1, source_target_pairs={{0,2},{1,3},{2,0},{3,1},{4,6},{5,7},{6,4},{7,5},{8,10},{9,11},{10,... | collective-permute-start | bytes 835592 | tf_op jit(solution)/shard_map/ppermute | solution.py:227
  15.3 1.3 %collective-permute-start.10 = (bf16[34,4,16,128]{3,2,1,0:T(8,128)(2,1)}, bf16[34,4,16,128]{3,2,1,0:T(8,128)(2,1)S(1)}, u32[]{:S(2)}, u32[]{:S(2)}) collective-permute-start(bf16[34,4,16,128]{3,2,1,0:T(8,128)(2,1)} %rights_0_.3), channel_id=1, source_target_pairs={{0,32},{16,48},{32,64},{48,80},{64,96},{80,112},{96,0},{112,16},{1... | collective-permute-start | bytes 1671176 | tf_op jit(solution)/shard_map/ppermute | solution.py:228
  16.6 17.8 %collective-permute-done.5.right = bf16[34,4,8,128]{3,2,1,0:T(8,128)(2,1)S(1)} collective-permute-done((bf16[34,4,8,128]{3,2,1,0:T(8,128)(2,1)}, bf16[34,4,8,128]{3,2,1,0:T(8,128)(2,1)S(1)}, u32[]{:S(2)}, u32[]{:S(2)}) %collective-permute-start.5) | collective-permute-done | bytes 278560 | tf_op jit(solution)/shard_map/ppermute | solution.py:227
  34.3 0.4 collective-permute-start.11
  34.8 2.9 %collective-permute-start.12 = (bf16[34,4,16,128]{3,2,1,0:T(8,128)(2,1)}, bf16[34,4,16,128]{3,2,1,0:T(8,128)(2,1)S(1)}, u32[]{:S(2)}, u32[]{:S(2)}) collective-permute-start(bf16[34,4,16,128]{3,2,1,0:T(8,128)(2,1)} %rights_0_.3), channel_id=1, source_target_pairs={{0,64},{16,80},{32,96},{48,112},{64,0},{80,16},{96,32},{112,48},{1... | collective-permute-start | bytes 1671176 | tf_op jit(solution)/shard_map/ppermute | solution.py:228
  37.7 1.1 copy-done.5
  38.9 0.9 shard_map.66
  39.8 1.5 %collective-permute-start.17 = (bf16[4,16,4,8,128]{4,3,2,1,0:T(8,128)(2,1)S(1)}, bf16[4,16,4,8,128]{4,3,2,1,0:T(8,128)(2,1)}, u32[]{:S(2)}, u32[]{:S(2)}) collective-permute-start(bf16[4,16,4,8,128]{4,3,2,1,0:T(8,128)(2,1)S(1)} %get-tuple-element.16.lefts_0_), channel_id=1, source_target_pairs={{0,4},{1,5},{2,6},{3,7},{4,8},{5,9},{6,10},{7,11},{8,12},{9,13},{1... | collective-permute-start | bytes 1572872 | tf_op jit(solution)/shard_map/ppermute | solution.py:233
  41.3 1.7 %collective-permute-start.8 = (bf16[4,18,4,8,128]{4,3,2,1,0:T(8,128)(2,1)}, bf16[4,18,4,8,128]{4,3,2,1,0:T(8,128)(2,1)}, u32[]{:S(2)}, u32[]{:S(2)}) collective-permute-start(bf16[4,18,4,8,128]{4,3,2,1,0:T(8,128)(2,1)} %get-tuple-element.15.lefts_0_), channel_id=1, source_target_pairs={{0,12},{1,13},{2,14},{3,15},{4,0},{5,1},{6,2},{7,3},{8,4},{9,5},{1... | collective-permute-start | bytes 1769480 | tf_op jit(solution)/shard_map/ppermute | solution.py:237
  43.0 4.7 %collective-permute-done.11.rights_2_ = bf16[34,4,16,128]{3,2,1,0:T(8,128)(2,1)S(1)} collective-permute-done((bf16[34,4,16,128]{3,2,1,0:T(8,128)(2,1)}, bf16[34,4,16,128]{3,2,1,0:T(8,128)(2,1)S(1)}, u32[]{:S(2)}, u32[]{:S(2)}) %collective-permute-start.11) | collective-permute-done | bytes 557088 | tf_op jit(solution)/shard_map/ppermute | solution.py:228
  47.8 1.2 %shard_map.65 = (bf16[8,2,256,128]{3,2,1,0:T(8,128)(2,1)}, bf16[8,2,256,128]{3,2,1,0:T(8,128)(2,1)S(1)}) custom-call(bf16[2,4,256,128]{3,2,1,0:T(8,128)(2,1)S(1)} %collective-permute-done.low_r, bf16[2,4,256,128]{3,2,1,0:T(8,128)(2,1)S(1)} %get-tuple-element.12.down, bf16[2,4,256,128]{3,2,1,0:T(8,128)(2,1)S(1)} %get-tuple-element.11.up, ...), custom_call_target="tpu_custom_call" | custom-call | flops 1048576 | bytes 4194304 | tf_op jit(solution)/shard_map/pallas_call | solution.py:67
  49.1 2.3 %collective-permute-start.2 = (bf16[8,2,256,128]{3,2,1,0:T(8,128)(2,1)}, bf16[8,2,256,128]{3,2,1,0:T(8,128)(2,1)}, u32[]{:S(2)}, u32[]{:S(2)}) collective-permute-start(bf16[8,2,256,128]{3,2,1,0:T(8,128)(2,1)} %get-tuple-element.13), channel_id=1, source_target_pairs={{0,16},{16,32},{32,48},{48,64},{64,80},{80,96},{96,112},{1,17},{17... | collective-permute-start | bytes 3145736 | tf_op jit(solution)/shard_map/ppermute | solution.py:224
  51.4 3.9 %collective-permute-done.17.lefts_1_ = bf16[4,16,4,8,128]{4,3,2,1,0:T(8,128)(2,1)} collective-permute-done((bf16[4,16,4,8,128]{4,3,2,1,0:T(8,128)(2,1)S(1)}, bf16[4,16,4,8,128]{4,3,2,1,0:T(8,128)(2,1)}, u32[]{:S(2)}, u32[]{:S(2)}) %collective-permute-start.17) | collective-permute-done | bytes 524320 | tf_op jit(solution)/shard_map/ppermute | solution.py:233
  55.2 5.0 %collective-permute-start.3 = (bf16[8,2,256,128]{3,2,1,0:T(8,128)(2,1)S(1)}, bf16[8,2,256,128]{3,2,1,0:T(8,128)(2,1)}, u32[]{:S(2)}, u32[]{:S(2)}) collective-permute-start(bf16[8,2,256,128]{3,2,1,0:T(8,128)(2,1)S(1)} %get-tuple-element.14), channel_id=1, source_target_pairs={{16,0},{32,16},{48,32},{64,48},{80,64},{96,80},{112,96},{17,1},{33... | collective-permute-start | bytes 3145736 | tf_op jit(solution)/shard_map/ppermute | solution.py:225
  60.2 7.7 %collective-permute-done.18.lefts_2_ = bf16[4,16,4,8,128]{4,3,2,1,0:T(8,128)(2,1)S(1)} collective-permute-done((bf16[4,16,4,8,128]{4,3,2,1,0:T(8,128)(2,1)S(1)}, bf16[4,16,4,8,128]{4,3,2,1,0:T(8,128)(2,1)S(1)}, u32[]{:S(2)}, u32[]{:S(2)}) %collective-permute-start.18) | collective-permute-done | bytes 524320 | tf_op jit(solution)/shard_map/ppermute | solution.py:234
  68.0 0.5 collective-permute-start.16
  68.5 1.3 %collective-permute-start.19 = (bf16[4,16,4,8,128]{4,3,2,1,0:T(8,128)(2,1)}, bf16[4,16,4,8,128]{4,3,2,1,0:T(8,128)(2,1)}, u32[]{:S(2)}, u32[]{:S(2)}) collective-permute-start(bf16[4,16,4,8,128]{4,3,2,1,0:T(8,128)(2,1)} %collective-permute-done.17.lefts_1_), channel_id=1, source_target_pairs={{0,4},{1,5},{2,6},{3,7},{4,8},{5,9},{6,10},{7,11},{8,12},{9,13},{1... | collective-permute-start | bytes 1572872 | tf_op jit(solution)/shard_map/ppermute | solution.py:235
  69.9 1.2 collective-permute-start.7
  71.2 0.8 copy-done.16
  72.0 2.5 %collective-permute-start.9 = (bf16[4,18,4,8,128]{4,3,2,1,0:T(8,128)(2,1)}, bf16[4,18,4,8,128]{4,3,2,1,0:T(8,128)(2,1)}, u32[]{:S(2)}, u32[]{:S(2)}) collective-permute-start(bf16[4,18,4,8,128]{4,3,2,1,0:T(8,128)(2,1)} %collective-permute-done.8.lefts_2_), channel_id=1, source_target_pairs={{0,12},{1,13},{2,14},{3,15},{4,0},{5,1},{6,2},{7,3},{8,4},{9,5},{1... | collective-permute-start | bytes 1769480 | tf_op jit(solution)/shard_map/ppermute | solution.py:238
  74.6 0.7 copy.8.shift
  75.3 9.6 %collective-permute-done.19.lefts_3_ = bf16[4,16,4,8,128]{4,3,2,1,0:T(8,128)(2,1)} collective-permute-done((bf16[4,16,4,8,128]{4,3,2,1,0:T(8,128)(2,1)}, bf16[4,16,4,8,128]{4,3,2,1,0:T(8,128)(2,1)}, u32[]{:S(2)}, u32[]{:S(2)}) %collective-permute-start.19) | collective-permute-done | bytes 524320 | tf_op jit(solution)/shard_map/ppermute | solution.py:235
  84.9 16.8 %shard_map.67.rest_0_ = f32[4,4,128,256]{3,2,1,0:T(8,128)} custom-call(s32[34,2]{1,0:T(8,128)} %copy.8.shift, s32[4]{0:T(128)} %left_size.5, s32[4]{0:T(128)} %right_size.5, bf16[2,4,256,128]{3,2,1,0:T(8,128)(2,1)} %copy-done.3, bf16[2,4,256,128]{3,2,1,0:T(8,128)(2,1)} %copy-done.1, bf16[2,4,256,128]{3,2,1,0:T(8,128)(2,1)} %copy-done.2, ...), custom_call_target="tpu_custom_call" | custom-call | flops 4294967296 | bytes 10485760 | tf_op jit(solution)/shard_map/pallas_call | solution.py:202
  101.8 18.9 %shard_map.68 = bf16[2,4,128,512]{3,2,1,0:T(8,128)(2,1)} custom-call(s32[34,2]{1,0:T(8,128)} %copy.8.shift, s32[4]{0:T(128)} %left_size.5, s32[4]{0:T(128)} %right_size.5, bf16[2,4,256,128]{3,2,1,0:T(8,128)(2,1)} %copy-done.3, bf16[2,4,256,128]{3,2,1,0:T(8,128)(2,1)} %copy-done.1, bf16[2,4,256,128]{3,2,1,0:T(8,128)(2,1)} %copy-done.2, ...), custom_call_target="tpu_custom_call" | custom-call | flops 4831838208 | bytes 10485760 | tf_op jit(solution)/shard_map/pallas_call | solution.py:202
  (50 shorter events, 0.4 us)
Async XLA Ops:
  0.0 15.3 %collective-permute-start.4 = (bf16[34,4,8,128]{3,2,1,0:T(8,128)(2,1)}, bf16[34,4,8,128]{3,2,1,0:T(8,128)(2,1)S(1)}, u32[]{:S(2)}, u32[]{:S(2)}) collective-permute-start(bf16[34,4,8,128]{3,2,1,0:T(8,128)(2,1)} %own.1), channel_id=1, source_target_pairs={{0,1},{1,2},{2,3},{3,0},{4,5},{5,6},{6,7},{7,4},{8,9},{9,10},{10,1... | collective-permute-start | bytes 835592 | tf_op jit(solution)/shard_map/ppermute | solution.py:227
  4.5 70.1 %copy-start.9 = (s32[34,2]{0,1:T(2,128)S(1)}, s32[34,2]{0,1:T(2,128)}, u32[]{:S(2)}) copy-start(s32[34,2]{0,1:T(2,128)} %param.11) | copy-start | bytes 820
  5.3 79.6 %copy-start.1 = (bf16[2,4,256,128]{3,2,1,0:T(8,128)(2,1)}, bf16[2,4,256,128]{3,2,1,0:T(8,128)(2,1)S(1)}, u32[]{:S(2)}) copy-start(bf16[2,4,256,128]{3,2,1,0:T(8,128)(2,1)S(1)} %get-tuple-element.12.down) | copy-start | bytes 1572868
  5.3 79.6 %copy-start.2 = (bf16[2,4,256,128]{3,2,1,0:T(8,128)(2,1)}, bf16[2,4,256,128]{3,2,1,0:T(8,128)(2,1)S(1)}, u32[]{:S(2)}) copy-start(bf16[2,4,256,128]{3,2,1,0:T(8,128)(2,1)S(1)} %get-tuple-element.11.up) | copy-start | bytes 1572868
  5.3 32.4 %collective-permute-start = (bf16[2,4,256,128]{3,2,1,0:T(8,128)(2,1)S(1)}, bf16[2,4,256,128]{3,2,1,0:T(8,128)(2,1)S(1)}, u32[]{:S(2)}, u32[]{:S(2)}) collective-permute-start(bf16[2,4,256,128]{3,2,1,0:T(8,128)(2,1)S(1)} %get-tuple-element.11.up), channel_id=1, source_target_pairs={{0,1},{1,2},{2,3},{3,4},{4,5},{5,6},{6,7},{7,8},{8,9},{9,10},{10,1... | collective-permute-start | bytes 1572872 | tf_op jit(solution)/shard_map/ppermute | solution.py:221
  9.2 25.2 %collective-permute-start.5 = (bf16[34,4,8,128]{3,2,1,0:T(8,128)(2,1)}, bf16[34,4,8,128]{3,2,1,0:T(8,128)(2,1)S(1)}, u32[]{:S(2)}, u32[]{:S(2)}) collective-permute-start(bf16[34,4,8,128]{3,2,1,0:T(8,128)(2,1)} %own.1), channel_id=1, source_target_pairs={{0,3},{1,0},{2,1},{3,2},{4,7},{5,4},{6,5},{7,6},{8,11},{9,8},{10,9... | collective-permute-start | bytes 835592 | tf_op jit(solution)/shard_map/ppermute | solution.py:227
  11.4 28.3 %collective-permute-start.1 = (bf16[2,4,256,128]{3,2,1,0:T(8,128)(2,1)S(1)}, bf16[2,4,256,128]{3,2,1,0:T(8,128)(2,1)S(1)}, u32[]{:S(2)}, u32[]{:S(2)}) collective-permute-start(bf16[2,4,256,128]{3,2,1,0:T(8,128)(2,1)S(1)} %get-tuple-element.12.down), channel_id=1, source_target_pairs={{1,0},{2,1},{3,2},{4,3},{5,4},{6,5},{7,6},{8,7},{9,8},{10,9},{11,1... | collective-permute-start | bytes 1572872 | tf_op jit(solution)/shard_map/ppermute | solution.py:222
  12.7 22.1 %collective-permute-start.6 = (bf16[34,4,8,128]{3,2,1,0:T(8,128)(2,1)}, bf16[34,4,8,128]{3,2,1,0:T(8,128)(2,1)S(1)}, u32[]{:S(2)}, u32[]{:S(2)}) collective-permute-start(bf16[34,4,8,128]{3,2,1,0:T(8,128)(2,1)} %own.1), channel_id=1, source_target_pairs={{0,2},{1,3},{2,0},{3,1},{4,6},{5,7},{6,4},{7,5},{8,10},{9,11},{10,... | collective-permute-start | bytes 835592 | tf_op jit(solution)/shard_map/ppermute | solution.py:227
  15.3 26.0 %collective-permute-start.10 = (bf16[34,4,16,128]{3,2,1,0:T(8,128)(2,1)}, bf16[34,4,16,128]{3,2,1,0:T(8,128)(2,1)S(1)}, u32[]{:S(2)}, u32[]{:S(2)}) collective-permute-start(bf16[34,4,16,128]{3,2,1,0:T(8,128)(2,1)} %rights_0_.3), channel_id=1, source_target_pairs={{0,32},{16,48},{32,64},{48,80},{64,96},{80,112},{96,0},{112,16},{1... | collective-permute-start | bytes 1671176 | tf_op jit(solution)/shard_map/ppermute | solution.py:228
  34.3 13.4 %collective-permute-start.11 = (bf16[34,4,16,128]{3,2,1,0:T(8,128)(2,1)}, bf16[34,4,16,128]{3,2,1,0:T(8,128)(2,1)S(1)}, u32[]{:S(2)}, u32[]{:S(2)}) collective-permute-start(bf16[34,4,16,128]{3,2,1,0:T(8,128)(2,1)} %rights_0_.3), channel_id=1, source_target_pairs={{0,96},{16,112},{32,0},{48,16},{64,32},{80,48},{96,64},{112,80},{1... | collective-permute-start | bytes 1671176 | tf_op jit(solution)/shard_map/ppermute | solution.py:228
  34.8 12.9 %collective-permute-start.12 = (bf16[34,4,16,128]{3,2,1,0:T(8,128)(2,1)}, bf16[34,4,16,128]{3,2,1,0:T(8,128)(2,1)S(1)}, u32[]{:S(2)}, u32[]{:S(2)}) collective-permute-start(bf16[34,4,16,128]{3,2,1,0:T(8,128)(2,1)} %rights_0_.3), channel_id=1, source_target_pairs={{0,64},{16,80},{32,96},{48,112},{64,0},{80,16},{96,32},{112,48},{1... | collective-permute-start | bytes 1671176 | tf_op jit(solution)/shard_map/ppermute | solution.py:228
  37.7 47.2 %copy-start.3 = (bf16[2,4,256,128]{3,2,1,0:T(8,128)(2,1)}, bf16[2,4,256,128]{3,2,1,0:T(8,128)(2,1)S(1)}, u32[]{:S(2)}) copy-start(bf16[2,4,256,128]{3,2,1,0:T(8,128)(2,1)S(1)} %collective-permute-done.low_r) | copy-start | bytes 1572868
  37.7 11.4 %collective-permute-start.13 = (bf16[34,4,16,128]{3,2,1,0:T(8,128)(2,1)}, bf16[34,4,16,128]{3,2,1,0:T(8,128)(2,1)S(1)}, u32[]{:S(2)}, u32[]{:S(2)}) collective-permute-start(bf16[34,4,16,128]{3,2,1,0:T(8,128)(2,1)} %rights_0_.3), channel_id=1, source_target_pairs={{0,16},{16,0},{32,48},{48,32},{64,80},{80,64},{96,112},{112,96},{1... | collective-permute-start | bytes 1671176 | tf_op jit(solution)/shard_map/ppermute | solution.py:230
  39.8 20.5 %copy-start.8 = (bf16[4,16,4,8,128]{4,3,2,1,0:T(8,128)(2,1)}, bf16[4,16,4,8,128]{4,3,2,1,0:T(8,128)(2,1)S(1)}, u32[]{:S(2)}) copy-start(bf16[4,16,4,8,128]{4,3,2,1,0:T(8,128)(2,1)S(1)} %get-tuple-element.16.lefts_0_) | copy-start | bytes 1572868
  39.8 45.2 %copy-start.4 = (bf16[2,4,256,128]{3,2,1,0:T(8,128)(2,1)}, bf16[2,4,256,128]{3,2,1,0:T(8,128)(2,1)S(1)}, u32[]{:S(2)}) copy-start(bf16[2,4,256,128]{3,2,1,0:T(8,128)(2,1)S(1)} %collective-permute-done.1.high_r) | copy-start | bytes 1572868
  39.8 15.5 %collective-permute-start.17 = (bf16[4,16,4,8,128]{4,3,2,1,0:T(8,128)(2,1)S(1)}, bf16[4,16,4,8,128]{4,3,2,1,0:T(8,128)(2,1)}, u32[]{:S(2)}, u32[]{:S(2)}) collective-permute-start(bf16[4,16,4,8,128]{4,3,2,1,0:T(8,128)(2,1)S(1)} %get-tuple-element.16.lefts_0_), channel_id=1, source_target_pairs={{0,4},{1,5},{2,6},{3,7},{4,8},{5,9},{6,10},{7,11},{8,12},{9,13},{1... | collective-permute-start | bytes 1572872 | tf_op jit(solution)/shard_map/ppermute | solution.py:233
  41.3 26.7 %copy-start.10 = (bf16[34,4,16,128]{3,2,1,0:T(8,128)(2,1)}, bf16[34,4,16,128]{3,2,1,0:T(8,128)(2,1)S(1)}, u32[]{:S(2)}) copy-start(bf16[34,4,16,128]{3,2,1,0:T(8,128)(2,1)S(1)} %collective-permute-done.10.rights_1_) | copy-start | bytes 1671172
  41.3 26.7 %collective-permute-start.8 = (bf16[4,18,4,8,128]{4,3,2,1,0:T(8,128)(2,1)}, bf16[4,18,4,8,128]{4,3,2,1,0:T(8,128)(2,1)}, u32[]{:S(2)}, u32[]{:S(2)}) collective-permute-start(bf16[4,18,4,8,128]{4,3,2,1,0:T(8,128)(2,1)} %get-tuple-element.15.lefts_0_), channel_id=1, source_target_pairs={{0,12},{1,13},{2,14},{3,15},{4,0},{5,1},{6,2},{7,3},{8,4},{9,5},{1... | collective-permute-start | bytes 1769480 | tf_op jit(solution)/shard_map/ppermute | solution.py:237
  47.7 20.8 %copy-start.11 = (bf16[34,4,16,128]{3,2,1,0:T(8,128)(2,1)}, bf16[34,4,16,128]{3,2,1,0:T(8,128)(2,1)S(1)}, u32[]{:S(2)}) copy-start(bf16[34,4,16,128]{3,2,1,0:T(8,128)(2,1)S(1)} %collective-permute-done.11.rights_2_) | copy-start | bytes 1671172
  47.7 20.3 %collective-permute-start.18 = (bf16[4,16,4,8,128]{4,3,2,1,0:T(8,128)(2,1)S(1)}, bf16[4,16,4,8,128]{4,3,2,1,0:T(8,128)(2,1)S(1)}, u32[]{:S(2)}, u32[]{:S(2)}) collective-permute-start(bf16[4,16,4,8,128]{4,3,2,1,0:T(8,128)(2,1)S(1)} %get-tuple-element.16.lefts_0_), channel_id=1, source_target_pairs={{0,12},{1,13},{2,14},{3,15},{4,0},{5,1},{6,2},{7,3},{8,4},{9,5},{1... | collective-permute-start | bytes 1572872 | tf_op jit(solution)/shard_map/ppermute | solution.py:234
  47.7 22.2 %copy-start.12 = (bf16[34,4,16,128]{3,2,1,0:T(8,128)(2,1)}, bf16[34,4,16,128]{3,2,1,0:T(8,128)(2,1)S(1)}, u32[]{:S(2)}) copy-start(bf16[34,4,16,128]{3,2,1,0:T(8,128)(2,1)S(1)} %collective-permute-done.12.rights_3_) | copy-start | bytes 1671172
  47.7 20.8 %collective-permute-start.14 = (bf16[34,4,16,128]{3,2,1,0:T(8,128)(2,1)S(1)}, bf16[34,4,16,128]{3,2,1,0:T(8,128)(2,1)S(1)}, u32[]{:S(2)}, u32[]{:S(2)}) collective-permute-start(bf16[34,4,16,128]{3,2,1,0:T(8,128)(2,1)S(1)} %collective-permute-done.10.rights_1_), channel_id=1, source_target_pairs={{0,16},{16,0},{32,48},{48,32},{64,80},{80,64},{96,112},{112,96},{1... | collective-permute-start | bytes 1671176 | tf_op jit(solution)/shard_map/ppermute | solution.py:230
  49.1 22.1 %copy-start.13 = (bf16[34,4,16,128]{3,2,1,0:T(8,128)(2,1)}, bf16[34,4,16,128]{3,2,1,0:T(8,128)(2,1)S(1)}, u32[]{:S(2)}) copy-start(bf16[34,4,16,128]{3,2,1,0:T(8,128)(2,1)S(1)} %collective-permute-done.13.partners_0_) | copy-start | bytes 1671172
  49.1 35.8 %collective-permute-start.2 = (bf16[8,2,256,128]{3,2,1,0:T(8,128)(2,1)}, bf16[8,2,256,128]{3,2,1,0:T(8,128)(2,1)}, u32[]{:S(2)}, u32[]{:S(2)}) collective-permute-start(bf16[8,2,256,128]{3,2,1,0:T(8,128)(2,1)} %get-tuple-element.13), channel_id=1, source_target_pairs={{0,16},{16,32},{32,48},{48,64},{64,80},{80,96},{96,112},{1,17},{17... | collective-permute-start | bytes 3145736 | tf_op jit(solution)/shard_map/ppermute | solution.py:224
  55.2 29.7 %collective-permute-start.3 = (bf16[8,2,256,128]{3,2,1,0:T(8,128)(2,1)S(1)}, bf16[8,2,256,128]{3,2,1,0:T(8,128)(2,1)}, u32[]{:S(2)}, u32[]{:S(2)}) collective-permute-start(bf16[8,2,256,128]{3,2,1,0:T(8,128)(2,1)S(1)} %get-tuple-element.14), channel_id=1, source_target_pairs={{16,0},{32,16},{48,32},{64,48},{80,64},{96,80},{112,96},{17,1},{33... | collective-permute-start | bytes 3145736 | tf_op jit(solution)/shard_map/ppermute | solution.py:225
  68.0 3.2 %copy-start.17 = (bf16[4,16,4,8,128]{4,3,2,1,0:T(8,128)(2,1)}, bf16[4,16,4,8,128]{4,3,2,1,0:T(8,128)(2,1)S(1)}, u32[]{:S(2)}) copy-start(bf16[4,16,4,8,128]{4,3,2,1,0:T(8,128)(2,1)S(1)} %collective-permute-done.18.lefts_2_) | copy-start | bytes 1572868
  68.0 2.0 %collective-permute-start.15 = (bf16[34,4,16,128]{3,2,1,0:T(8,128)(2,1)S(1)}, bf16[34,4,16,128]{3,2,1,0:T(8,128)(2,1)S(1)}, u32[]{:S(2)}, u32[]{:S(2)}) collective-permute-start(bf16[34,4,16,128]{3,2,1,0:T(8,128)(2,1)S(1)} %collective-permute-done.11.rights_2_), channel_id=1, source_target_pairs={{0,16},{16,0},{32,48},{48,32},{64,80},{80,64},{96,112},{112,96},{1... | collective-permute-start | bytes 1671176 | tf_op jit(solution)/shard_map/ppermute | solution.py:230
  68.0 3.1 %collective-permute-start.16 = (bf16[34,4,16,128]{3,2,1,0:T(8,128)(2,1)S(1)}, bf16[34,4,16,128]{3,2,1,0:T(8,128)(2,1)S(1)}, u32[]{:S(2)}, u32[]{:S(2)}) collective-permute-start(bf16[34,4,16,128]{3,2,1,0:T(8,128)(2,1)S(1)} %collective-permute-done.12.rights_3_), channel_id=1, source_target_pairs={{0,16},{16,0},{32,48},{48,32},{64,80},{80,64},{96,112},{112,96},{1... | collective-permute-start | bytes 1671176 | tf_op jit(solution)/shard_map/ppermute | solution.py:230
  68.5 2.7 %copy-start.14 = (bf16[34,4,16,128]{3,2,1,0:T(8,128)(2,1)}, bf16[34,4,16,128]{3,2,1,0:T(8,128)(2,1)S(1)}, u32[]{:S(2)}) copy-start(bf16[34,4,16,128]{3,2,1,0:T(8,128)(2,1)S(1)} %collective-permute-done.14.partners_1_) | copy-start | bytes 1671172
  68.5 16.4 %collective-permute-start.19 = (bf16[4,16,4,8,128]{4,3,2,1,0:T(8,128)(2,1)}, bf16[4,16,4,8,128]{4,3,2,1,0:T(8,128)(2,1)}, u32[]{:S(2)}, u32[]{:S(2)}) collective-permute-start(bf16[4,16,4,8,128]{4,3,2,1,0:T(8,128)(2,1)} %collective-permute-done.17.lefts_1_), channel_id=1, source_target_pairs={{0,4},{1,5},{2,6},{3,7},{4,8},{5,9},{6,10},{7,11},{8,12},{9,13},{1... | collective-permute-start | bytes 1572872 | tf_op jit(solution)/shard_map/ppermute | solution.py:235
  69.9 31.8 %collective-permute-start.7 = (bf16[4,18,4,8,128]{4,3,2,1,0:T(8,128)(2,1)}, bf16[4,18,4,8,128]{4,3,2,1,0:T(8,128)(2,1)}, u32[]{:S(2)}, u32[]{:S(2)}) collective-permute-start(bf16[4,18,4,8,128]{4,3,2,1,0:T(8,128)(2,1)} %get-tuple-element.15.lefts_0_), channel_id=1, source_target_pairs={{0,4},{1,5},{2,6},{3,7},{4,8},{5,9},{6,10},{7,11},{8,12},{9,13},{1... | collective-permute-start | bytes 1769480 | tf_op jit(solution)/shard_map/ppermute | solution.py:236
  72.0 29.8 %collective-permute-start.9 = (bf16[4,18,4,8,128]{4,3,2,1,0:T(8,128)(2,1)}, bf16[4,18,4,8,128]{4,3,2,1,0:T(8,128)(2,1)}, u32[]{:S(2)}, u32[]{:S(2)}) collective-permute-start(bf16[4,18,4,8,128]{4,3,2,1,0:T(8,128)(2,1)} %collective-permute-done.8.lefts_2_), channel_id=1, source_target_pairs={{0,12},{1,13},{2,14},{3,15},{4,0},{5,1},{6,2},{7,3},{8,4},{9,5},{1... | collective-permute-start | bytes 1769480 | tf_op jit(solution)/shard_map/ppermute | solution.py:238
  (6 other events, 5.7 us)

commit v3 on v2

--- a/solution.py
+++ b/solution.py
@@ -7,9 +7,11 @@
 from jax.experimental.pallas import tpu as pltpu
 from jax.sharding import PartitionSpec as P
 
+
 KCH = 34
 SHIFT = 2
 SPLIT = 16
+STAGED = 4
 XN, ZN, YN, CORES = 4, 4, 4, 2
 NT = (((1,), (1,)), ((), ()))
 NN = (((1,), (0,)), ((), ()))
@@ -74,24 +76,39 @@
     )(low_r, down, up, high_r)
 
 
-def bundle_kernel(own, left, right, far, first, second):
+def split_kernel(whole, first, second):
+    first[...] = whole[:SPLIT]
+    second[...] = whole[SPLIT:]
+
+
+def split_channels(left_env):
+    vmem = pl.BlockSpec(memory_space=pltpu.VMEM)
+    return pl.pallas_call(
+        split_kernel,
+        out_shape=tuple(
+            jax.ShapeDtypeStruct((many, 4, 8, 128), jnp.bfloat16) for many in (SPLIT, KCH - SPLIT)
+        ),
+        in_specs=[vmem],
+        out_specs=(vmem, vmem),
+        compiler_params=pltpu.CompilerParams(vmem_limit_bytes=8 << 20),
+        cost_estimate=pl.CostEstimate(flops=1 << 20, bytes_accessed=1 << 20, transcendentals=0),
+    )(left_env)
+
+
+def bundle_kernel(own, left, right, far, out):
     for at, part in enumerate((own, left, right, far)):
-        first[at] = part[:SPLIT]
-        second[at] = part[SPLIT:]
+        out[at] = part[...]
 
 
 def bundled(own, left, right, far):
     vmem = pl.BlockSpec(memory_space=pltpu.VMEM)
     return pl.pallas_call(
         bundle_kernel,
-        out_shape=tuple(
-            jax.ShapeDtypeStruct((4, many, 4, 8, 128), jnp.bfloat16)
-            for many in (SPLIT, KCH - SPLIT)
-        ),
+        out_shape=jax.ShapeDtypeStruct((4, *own.shape), jnp.bfloat16),
         in_specs=[vmem] * 4,
-        out_specs=(vmem, vmem),
+        out_specs=vmem,
         compiler_params=pltpu.CompilerParams(vmem_limit_bytes=8 << 20),
-        cost_estimate=pl.CostEstimate(flops=1 << 20, bytes_accessed=2 << 20, transcendentals=0),
+        cost_estimate=pl.CostEstimate(flops=1 << 20, bytes_accessed=1 << 20, transcendentals=0),
     )(own, left, right, far)
 
 
@@ -107,39 +124,45 @@
     out = rest.pop(0)
     source, left_all, right_all = rest[:3]
     rest = rest[3:]
-    total = rest.pop(0) if is_last else out
+    total, carried = (rest.pop(0), rest.pop(0)) if is_last else (out, None)
     sems = rest.pop(0)
     rsec, lsec = lax.axis_index("rsec"), lax.axis_index("lsec")
     x, z, y, core = rsec // ZN, lax.rem(rsec, ZN), lsec // CORES, lax.rem(lsec, CORES)
 
-    copies = []
+    waits = []
 
     def start(src, dst):
-        copy = pltpu.make_async_copy(src, dst, sems.at[len(copies)])
+        copy = pltpu.make_async_copy(src, dst, sems.at[len(waits)])
         copy.start()
-        copies.append(copy)
+        waits.append(copy)
 
     for at, part in enumerate((low_r, down, up, high_r)):
         start(part, source.at[2 * at : 2 * at + 2, 2:6])
     start(low_l, source.at[:, 0:2])
     start(high_l, source.at[:, 6:8])
-    for step, own, other in zip(RING_STEPS, rights, partners):
-        for part, side in ((own, core), (other, 1 - core)):
-            row = pl.multiple_of(16 * (CORES * lax.rem(y + step + YN, YN) + side), 16)
-            start(part.at[first : first + count], right_all.at[:, :, pl.ds(row, 16)])
-    for dx, bundle in zip(RING_STEPS, lefts):
-        for at, dz in enumerate(RING_STEPS):
-            row = 8 * (ZN * lax.rem(x + dx + XN, XN) + lax.rem(z + dz + ZN, ZN))
-            start(bundle.at[at], left_all.at[:, :, pl.ds(pl.multiple_of(row, 8), 8)])
-    if is_first:
-        total[...] = jnp.zeros_like(total)
-    else:
-        start(total_in, total)
-    for copy in copies:
-        copy.wait()
-
-    def two_channels(pair, carry):
-        ks = (2 * pair, 2 * pair + 1)
+    ready = []
+    for begin, end in ((0, STAGED), (STAGED, count)):
+        for step, own, other in zip(RING_STEPS, rights, partners):
+            for part, side in ((own, core), (other, 1 - core)):
+                row = pl.multiple_of(16 * (CORES * lax.rem(y + step + YN, YN) + side), 16)
+                start(
+                    part.at[first + begin : first + end],
+                    right_all.at[begin:end, :, pl.ds(row, 16)],
+                )
+        for outer, bundle in zip(RING_STEPS, lefts):
+            for at, inner in enumerate(RING_STEPS):
+                dx, dz = (outer, inner) if is_first else (inner, outer)
+                row = 8 * (ZN * lax.rem(x + dx + XN, XN) + lax.rem(z + dz + ZN, ZN))
+                start(
+                    bundle.at[at, begin:end],
+                    left_all.at[begin:end, :, pl.ds(pl.multiple_of(row, 8), 8)],
+                )
+        ready.append(len(waits))
+    if not is_first:
+        start(total_in, carried)
+    total[...] = jnp.zeros_like(total)
+
+    def add_channels(ks):
         shifts = [(shift[first + k, 0], shift[first + k, 1]) for k in ks]
         for r in range(4):
             partial = []
@@ -151,22 +174,39 @@
                     ).astype(jnp.bfloat16)
                 )
             for l in range(4):
-                stacked = jnp.concatenate(
-                    [
-                        jnp.concatenate(
-                            [p[l * 256 : l * 256 + 128], p[l * 256 + 128 : l * 256 + 256]], axis=1
-                        )
-                        for p in partial
-                    ],
-                    axis=0,
-                )
-                sides = jnp.concatenate([left_all[k, l] for k in ks], axis=1)
-                total[l, r] += lax.dot_general(
-                    sides, stacked, NN, preferred_element_type=jnp.float32
-                )
+                added = None
+                for at in range(0, len(ks), 2):
+                    stacked = jnp.concatenate(
+                        [
+                            jnp.concatenate(
+                                [p[l * 256 : l * 256 + 128], p[l * 256 + 128 : l * 256 + 256]],
+                                axis=1,
+                            )
+                            for p in partial[at : at + 2]
+                        ],
+                        axis=0,
+                    )
+                    sides = jnp.concatenate([left_all[k, l] for k in ks[at : at + 2]], axis=1)
+                    product = lax.dot_general(
+                        sides, stacked, NN, preferred_element_type=jnp.float32
+                    )
+                    added = product if added is None else added + product
+                total[l, r] += added
+
+    def four_channels(group, carry):
+        add_channels([4 * group + j for j in range(4)])
         return carry
 
-    lax.fori_loop(0, count // 2, two_channels, 0)
+    for copy in waits[: ready[0]]:
+        copy.wait()
+    add_channels(list(range(STAGED)))
+    for copy in waits[ready[0] : ready[1]]:
+        copy.wait()
+    lax.fori_loop(1, count // 4, four_channels, 0)
+    if count % 4:
+        add_channels(list(range(count // 4 * 4, count)))
+    for copy in waits[ready[1] :]:
+        copy.wait()
 
     if is_last:
         row = lax.broadcasted_iota(jnp.int32, (128, 128), 0)
@@ -175,7 +215,8 @@
             for r in range(4):
                 live = (row < left_size[l]) & (col < right_size[r])
                 for v in range(2):
-                    block = total[l, r, :, v * 128 : v * 128 + 128]
+                    lanes = slice(v * 128, v * 128 + 128)
+                    block = total[l, r, :, lanes] + carried[l, r, :, lanes]
                     out[v, l, :, r * 128 : r * 128 + 128] = jnp.where(live, block, 0.0).astype(
                         jnp.bfloat16
                     )
@@ -197,8 +238,8 @@
         pltpu.VMEM((count, 4, 128, 128), jnp.bfloat16),
     ]
     if is_last:
-        scratch.append(pltpu.VMEM((4, 4, 128, 256), jnp.float32))
-    scratch.append(pltpu.SemaphoreType.DMA((40,)))
+        scratch += [pltpu.VMEM((4, 4, 128, 256), jnp.float32)] * 2
+    scratch.append(pltpu.SemaphoreType.DMA((56,)))
     return pl.pallas_call(
         functools.partial(channels_kernel, first, count, is_first, is_last),
         out_shape=result if is_last else totals,
@@ -212,7 +253,13 @@
     )(*operands)
 
 
-def local(two_site, left_env, right_env, left_size, right_size, channel_shift):
+def applied(two_site, left_env, right_env, left_size, right_size, channel_shift):
+    steps = (1, -1, 2)
+    rights = [right_env] + [lax.ppermute(right_env, "lsec", shifted_y(steps[i])) for i in range(3)]
+    part_a, part_b = split_channels(left_env)
+    ring_a = [lax.ppermute(part_a, "rsec", shifted_z(steps[i])) for i in range(3)]
+    ring_b = [lax.ppermute(part_b, "rsec", shifted_x(steps[i])) for i in range(3)]
+
     down, up = masked_halves(two_site, left_size, right_size)
     l_up = [(i, i + 1) for i in range(7)]
     l_down = [(i + 1, i) for i in range(7)]
@@ -220,32 +267,24 @@
     r_down = [(i + 1, i) for i in range(15)]
     low_r = lax.ppermute(up, "rsec", r_up)
     high_r = lax.ppermute(down, "rsec", r_down)
+
+    bundle_a = bundled(part_a, *ring_a)
+    lefts_a = [bundle_a] + [lax.ppermute(bundle_a, "rsec", shifted_x(steps[i])) for i in range(3)]
     to_next, to_previous = left_rims(low_r, down, up, high_r)
     low_l = lax.ppermute(to_next, "lsec", l_up)
     high_l = lax.ppermute(to_previous, "lsec", l_down)
 
-    z_ring = [lax.ppermute(left_env, "rsec", shifted_z(step)) for step in (1, -1, 2)]
-    rights = [right_env] + [lax.ppermute(right_env, "lsec", shifted_y(s)) for s in (1, -1, 2)]
     swap = [(i, i ^ 1) for i in range(8)]
     partners = [lax.ppermute(part, "lsec", swap) for part in rights]
 
-    bundle_a, bundle_b = bundled(left_env, *z_ring)
-    left_a = lax.ppermute(bundle_a, "rsec", shifted_x(1))
-    right_a = lax.ppermute(bundle_a, "rsec", shifted_x(-1))
-    far_a = lax.ppermute(left_a, "rsec", shifted_x(1))
-    left_b = lax.ppermute(bundle_b, "rsec", shifted_x(1))
-    right_b = lax.ppermute(bundle_b, "rsec", shifted_x(-1))
-    far_b = lax.ppermute(right_b, "rsec", shifted_x(-1))
+    bundle_b = bundled(part_b, *ring_b)
+    lefts_b = [bundle_b] + [lax.ppermute(bundle_b, "rsec", shifted_z(steps[i])) for i in range(3)]
 
     scalars = (channel_shift, left_size, right_size)
     sources = (low_r, down, up, high_r, low_l, high_l)
-    lefts_a = (bundle_a, left_a, right_a, far_a)
-    lefts_b = (bundle_b, left_b, right_b, far_b)
-    total = run_channels(
-        0, SPLIT, True, False, scalars, sources, lefts_a, rights, partners, None
-    )
+    total = run_channels(0, SPLIT, True, False, scalars, sources, lefts_a, rights, partners, None)
     return run_channels(
-        SPLIT, KCH - SPLIT, False, True, scalars, sources, lefts_b, rights, partners, total
+        SPLIT, KCH - SPLIT, False, True, scalars, sources, lefts_b, rights, partners, total,
     )
 
 
@@ -259,5 +298,5 @@
         P(),
     )
     return jax.shard_map(
-        local, mesh=mesh, in_specs=placed, out_specs=P(None, "lsec", None, "rsec"), check_vma=False
+        applied, mesh=mesh, in_specs=placed, out_specs=P(None, "lsec", None, "rsec"), check_vma=False
     )

time: 122 us -> 125 us (1.025)
  the two profiles are of different devices: /device:TPU:16 before, /device:TPU:1 now
where the time goes in v3:
time: 125 us
  starting transfers between devices  62.5 us (50%)
  Pallas kernels  30.5 us (24%)
  waiting for transfers between devices  24.9 us (20%)
  local copies, waits for them, and re-layouts  6.1 us (5%)
    pallas_call x2, Pallas kernels, run_channels(): pl.pallas_call(functools.partial(channels_kernel, first, count, is_first,...  28.2 us
    ppermute x4, starting transfers between devices, applied(): partners = [lax.ppermute(part, 'lsec', swap) for part in rights]  15.2 us
    ppermute x3, starting transfers between devices, applied(): lax.ppermute(part_b, 'rsec', shifted_x(steps[i]))  11.4 us
    ppermute x3, starting transfers between devices, applied(): lax.ppermute(bundle_a, 'rsec', shifted_x(steps[i]))  11.2 us
    ppermute x3, waiting for transfers between devices, applied(): lax.ppermute(bundle_b, 'rsec', shifted_z(steps[i]))  11 us
    ppermute x3, waiting for transfers between devices, applied(): lax.ppermute(part_a, 'rsec', shifted_z(steps[i]))  6.37 us
    unnamed x47, local copies, waits for them, and re-layouts  6.1 us
    ppermute x3, starting transfers between devices, applied(): lax.ppermute(part_a, 'rsec', shifted_z(steps[i]))  4.81 us
  transfers between devices with their start and end apart: 23, of which 6 were waited for; matrix products, arithmetic and copies ran while one was open for 1% of the time, Pallas kernels for 12%

profile of v3, /device:TPU:1, one launch (start us, length us, event | category | flops | bytes accessed | tf_op | source)
XLA Modules:
  0.0 124.5 jit_solution(11471398910661009609)
XLA Ops:
  0.0 1.2 copy-done
  3.4 4.4 %collective-permute-start = (bf16[2,4,256,128]{3,2,1,0:T(8,128)(2,1)S(1)}, bf16[2,4,256,128]{3,2,1,0:T(8,128)(2,1)S(1)}, u32[]{:S(2)}, u32[]{:S(2)}) collective-permute-start(bf16[2,4,256,128]{3,2,1,0:T(8,128)(2,1)S(1)} %get-tuple-element.11.up), channel_id=1, source_target_pairs={{0,1},{1,2},{2,3},{3,4},{4,5},{5,6},{6,7},{7,8},{8,9},{9,10},{10,1... | collective-permute-start | bytes 1572872 | tf_op jit(solution)/shard_map/ppermute | solution.py:268
  7.8 0.9 copy-done.7
  8.8 1.7 %collective-permute-start.17 = (bf16[16,4,8,128]{3,2,1,0:T(8,128)(2,1)S(1)}, bf16[16,4,8,128]{3,2,1,0:T(8,128)(2,1)S(1)}, u32[]{:S(2)}, u32[]{:S(2)}) collective-permute-start(bf16[16,4,8,128]{3,2,1,0:T(8,128)(2,1)S(1)} %get-tuple-element.16.own), channel_id=1, source_target_pairs={{0,1},{1,2},{2,3},{3,0},{4,5},{5,6},{6,7},{7,4},{8,9},{9,10},{10,1... | collective-permute-start | bytes 393224 | tf_op jit(solution)/shard_map/ppermute | solution.py:260
  10.4 1.1 collective-permute-start.18
  11.5 2.1 %collective-permute-start.19 = (bf16[16,4,8,128]{3,2,1,0:T(8,128)(2,1)S(1)}, bf16[16,4,8,128]{3,2,1,0:T(8,128)(2,1)S(1)}, u32[]{:S(2)}, u32[]{:S(2)}) collective-permute-start(bf16[16,4,8,128]{3,2,1,0:T(8,128)(2,1)S(1)} %get-tuple-element.16.own), channel_id=1, source_target_pairs={{0,2},{1,3},{2,0},{3,1},{4,6},{5,7},{6,4},{7,5},{8,10},{9,11},{10,... | collective-permute-start | bytes 393224 | tf_op jit(solution)/shard_map/ppermute | solution.py:260
  13.6 1.2 collective-permute-start.4
  14.8 6.4 %collective-permute-done.17.left = bf16[16,4,8,128]{3,2,1,0:T(8,128)(2,1)S(1)} collective-permute-done((bf16[16,4,8,128]{3,2,1,0:T(8,128)(2,1)S(1)}, bf16[16,4,8,128]{3,2,1,0:T(8,128)(2,1)S(1)}, u32[]{:S(2)}, u32[]{:S(2)}) %collective-permute-start.17) | collective-permute-done | bytes 131104 | tf_op jit(solution)/shard_map/ppermute | solution.py:260
  21.1 6.8 %collective-permute-start.5 = (bf16[18,4,8,128]{3,2,1,0:T(8,128)(2,1)S(1)}, bf16[18,4,8,128]{3,2,1,0:T(8,128)(2,1)S(1)}, u32[]{:S(2)}, u32[]{:S(2)}) collective-permute-start(bf16[18,4,8,128]{3,2,1,0:T(8,128)(2,1)S(1)} %get-tuple-element.15.own), channel_id=1, source_target_pairs={{0,12},{1,13},{2,14},{3,15},{4,0},{5,1},{6,2},{7,3},{8,4},{9,5},{1... | collective-permute-start | bytes 442376 | tf_op jit(solution)/shard_map/ppermute | solution.py:261
  27.9 1.3 %collective-permute-start.10 = (bf16[34,4,16,128]{3,2,1,0:T(8,128)(2,1)}, bf16[34,4,16,128]{3,2,1,0:T(8,128)(2,1)S(1)}, u32[]{:S(2)}, u32[]{:S(2)}) collective-permute-start(bf16[34,4,16,128]{3,2,1,0:T(8,128)(2,1)} %rights_0_.3), channel_id=1, source_target_pairs={{0,32},{16,48},{32,64},{48,80},{64,96},{80,112},{96,0},{112,16},{1... | collective-permute-start | bytes 1671176 | tf_op jit(solution)/shard_map/ppermute | solution.py:258
  29.2 1.5 %collective-permute-start.11 = (bf16[34,4,16,128]{3,2,1,0:T(8,128)(2,1)}, bf16[34,4,16,128]{3,2,1,0:T(8,128)(2,1)S(1)}, u32[]{:S(2)}, u32[]{:S(2)}) collective-permute-start(bf16[34,4,16,128]{3,2,1,0:T(8,128)(2,1)} %rights_0_.3), channel_id=1, source_target_pairs={{0,96},{16,112},{32,0},{48,16},{64,32},{80,48},{96,64},{112,80},{1... | collective-permute-start | bytes 1671176 | tf_op jit(solution)/shard_map/ppermute | solution.py:258
  30.7 1.4 %collective-permute-start.1 = (bf16[2,4,256,128]{3,2,1,0:T(8,128)(2,1)S(1)}, bf16[2,4,256,128]{3,2,1,0:T(8,128)(2,1)S(1)}, u32[]{:S(2)}, u32[]{:S(2)}) collective-permute-start(bf16[2,4,256,128]{3,2,1,0:T(8,128)(2,1)S(1)} %get-tuple-element.12.down), channel_id=1, source_target_pairs={{1,0},{2,1},{3,2},{4,3},{5,4},{6,5},{7,6},{8,7},{9,8},{10,9},{11,1... | collective-permute-start | bytes 1572872 | tf_op jit(solution)/shard_map/ppermute | solution.py:269
  32.2 3.4 %collective-permute-start.6 = (bf16[18,4,8,128]{3,2,1,0:T(8,128)(2,1)S(1)}, bf16[18,4,8,128]{3,2,1,0:T(8,128)(2,1)S(1)}, u32[]{:S(2)}, u32[]{:S(2)}) collective-permute-start(bf16[18,4,8,128]{3,2,1,0:T(8,128)(2,1)S(1)} %get-tuple-element.15.own), channel_id=1, source_target_pairs={{0,8},{1,9},{2,10},{3,11},{4,12},{5,13},{6,14},{7,15},{8,0},{9,1},... | collective-permute-start | bytes 442376 | tf_op jit(solution)/shard_map/ppermute | solution.py:261
  35.6 2.5 %collective-permute-done.6.far = bf16[18,4,8,128]{3,2,1,0:T(8,128)(2,1)S(1)} collective-permute-done((bf16[18,4,8,128]{3,2,1,0:T(8,128)(2,1)S(1)}, bf16[18,4,8,128]{3,2,1,0:T(8,128)(2,1)S(1)}, u32[]{:S(2)}, u32[]{:S(2)}) %collective-permute-start.6) | collective-permute-done | bytes 147488 | tf_op jit(solution)/shard_map/ppermute | solution.py:261
  38.1 1.2 collective-permute-start.12
  39.3 3.1 %collective-permute-start.13 = (bf16[34,4,16,128]{3,2,1,0:T(8,128)(2,1)}, bf16[34,4,16,128]{3,2,1,0:T(8,128)(2,1)S(1)}, u32[]{:S(2)}, u32[]{:S(2)}) collective-permute-start(bf16[34,4,16,128]{3,2,1,0:T(8,128)(2,1)} %rights_0_.3), channel_id=1, source_target_pairs={{0,16},{16,0},{32,48},{48,32},{64,80},{80,64},{96,112},{112,96},{1... | collective-permute-start | bytes 1671176 | tf_op jit(solution)/shard_map/ppermute | solution.py:278
  42.5 1.9 %collective-permute-done.1.high_r = bf16[2,4,256,128]{3,2,1,0:T(8,128)(2,1)S(1)} collective-permute-done((bf16[2,4,256,128]{3,2,1,0:T(8,128)(2,1)S(1)}, bf16[2,4,256,128]{3,2,1,0:T(8,128)(2,1)S(1)}, u32[]{:S(2)}, u32[]{:S(2)}) %collective-permute-start.1) | collective-permute-done | bytes 524320 | tf_op jit(solution)/shard_map/ppermute | solution.py:269
  44.4 8.2 %collective-permute-start.20 = (bf16[4,16,4,8,128]{4,3,2,1,0:T(8,128)(2,1)S(1)}, bf16[4,16,4,8,128]{4,3,2,1,0:T(8,128)(2,1)S(1)}, u32[]{:S(2)}, u32[]{:S(2)}) collective-permute-start(bf16[4,16,4,8,128]{4,3,2,1,0:T(8,128)(2,1)S(1)} %shard_map.68.lefts_0_), channel_id=1, source_target_pairs={{0,4},{1,5},{2,6},{3,7},{4,8},{5,9},{6,10},{7,11},{8,12},{9,13},{1... | collective-permute-start | bytes 1572872 | tf_op jit(solution)/shard_map/ppermute | solution.py:272
  52.6 1.9 %collective-permute-start.21 = (bf16[4,16,4,8,128]{4,3,2,1,0:T(8,128)(2,1)S(1)}, bf16[4,16,4,8,128]{4,3,2,1,0:T(8,128)(2,1)S(1)}, u32[]{:S(2)}, u32[]{:S(2)}) collective-permute-start(bf16[4,16,4,8,128]{4,3,2,1,0:T(8,128)(2,1)S(1)} %shard_map.68.lefts_0_), channel_id=1, source_target_pairs={{0,12},{1,13},{2,14},{3,15},{4,0},{5,1},{6,2},{7,3},{8,4},{9,5},{1... | collective-permute-start | bytes 1572872 | tf_op jit(solution)/shard_map/ppermute | solution.py:272
  54.5 1.2 collective-permute-start.22
  55.7 1.5 %shard_map.65 = (bf16[8,2,256,128]{3,2,1,0:T(8,128)(2,1)}, bf16[8,2,256,128]{3,2,1,0:T(8,128)(2,1)}) custom-call(bf16[2,4,256,128]{3,2,1,0:T(8,128)(2,1)S(1)} %collective-permute-done.low_r, bf16[2,4,256,128]{3,2,1,0:T(8,128)(2,1)S(1)} %get-tuple-element.12.down, bf16[2,4,256,128]{3,2,1,0:T(8,128)(2,1)S(1)} %get-tuple-element.11.up, ...), custom_call_target="tpu_custom_call" | custom-call | flops 1048576 | bytes 4194304 | tf_op jit(solution)/shard_map/pallas_call | solution.py:69
  57.1 3.1 %collective-permute-start.2 = (bf16[8,2,256,128]{3,2,1,0:T(8,128)(2,1)}, bf16[8,2,256,128]{3,2,1,0:T(8,128)(2,1)}, u32[]{:S(2)}, u32[]{:S(2)}) collective-permute-start(bf16[8,2,256,128]{3,2,1,0:T(8,128)(2,1)} %get-tuple-element.13), channel_id=1, source_target_pairs={{0,16},{16,32},{32,48},{48,64},{64,80},{80,96},{96,112},{1,17},{17... | collective-permute-start | bytes 3145736 | tf_op jit(solution)/shard_map/ppermute | solution.py:274
  60.2 4.2 %collective-permute-start.3 = (bf16[8,2,256,128]{3,2,1,0:T(8,128)(2,1)}, bf16[8,2,256,128]{3,2,1,0:T(8,128)(2,1)}, u32[]{:S(2)}, u32[]{:S(2)}) collective-permute-start(bf16[8,2,256,128]{3,2,1,0:T(8,128)(2,1)} %get-tuple-element.14), channel_id=1, source_target_pairs={{16,0},{32,16},{48,32},{64,48},{80,64},{96,80},{112,96},{17,1},{33... | collective-permute-start | bytes 3145736 | tf_op jit(solution)/shard_map/ppermute | solution.py:275
  64.5 2.2 %collective-permute-done.20.lefts_1_ = bf16[4,16,4,8,128]{4,3,2,1,0:T(8,128)(2,1)S(1)} collective-permute-done((bf16[4,16,4,8,128]{4,3,2,1,0:T(8,128)(2,1)S(1)}, bf16[4,16,4,8,128]{4,3,2,1,0:T(8,128)(2,1)S(1)}, u32[]{:S(2)}, u32[]{:S(2)}) %collective-permute-start.20) | collective-permute-done | bytes 524320 | tf_op jit(solution)/shard_map/ppermute | solution.py:272
  67.3 10.6 %collective-permute-start.15 = (bf16[34,4,16,128]{3,2,1,0:T(8,128)(2,1)S(1)}, bf16[34,4,16,128]{3,2,1,0:T(8,128)(2,1)S(1)}, u32[]{:S(2)}, u32[]{:S(2)}) collective-permute-start(bf16[34,4,16,128]{3,2,1,0:T(8,128)(2,1)S(1)} %collective-permute-done.11.rights_2_), channel_id=1, source_target_pairs={{0,16},{16,0},{32,48},{48,32},{64,80},{80,64},{96,112},{112,96},{1... | collective-permute-start | bytes 1671176 | tf_op jit(solution)/shard_map/ppermute | solution.py:278
  77.9 0.9 collective-permute-done.22.lefts_3_
  78.8 0.9 collective-permute-start.16
  79.9 2.6 %collective-permute-start.8 = (bf16[4,18,4,8,128]{4,3,2,1,0:T(8,128)(2,1)S(1)}, bf16[4,18,4,8,128]{4,3,2,1,0:T(8,128)(2,1)S(1)}, u32[]{:S(2)}, u32[]{:S(2)}) collective-permute-start(bf16[4,18,4,8,128]{4,3,2,1,0:T(8,128)(2,1)S(1)} %shard_map.67.lefts_0_), channel_id=1, source_target_pairs={{0,3},{1,0},{2,1},{3,2},{4,7},{5,4},{6,5},{7,6},{8,11},{9,8},{10,9... | collective-permute-start | bytes 1769480 | tf_op jit(solution)/shard_map/ppermute | solution.py:281
  84.1 13.5 %shard_map.69.rest_0_ = f32[4,4,128,256]{3,2,1,0:T(8,128)} custom-call(s32[34,2]{1,0:T(8,128)} %copy.8.shift, s32[4]{0:T(128)} %left_size.5, s32[4]{0:T(128)} %right_size.5, bf16[2,4,256,128]{3,2,1,0:T(8,128)(2,1)} %copy-done.5, bf16[2,4,256,128]{3,2,1,0:T(8,128)(2,1)} %copy-done.3, bf16[2,4,256,128]{3,2,1,0:T(8,128)(2,1)} %copy-done.4, ...), custom_call_target="tpu_custom_call" | custom-call | flops 4294967296 | bytes 10485760 | tf_op jit(solution)/shard_map/pallas_call | solution.py:243
  97.6 11.0 %collective-permute-done.7.lefts_1_ = bf16[4,18,4,8,128]{4,3,2,1,0:T(8,128)(2,1)S(1)} collective-permute-done((bf16[4,18,4,8,128]{4,3,2,1,0:T(8,128)(2,1)S(1)}, bf16[4,18,4,8,128]{4,3,2,1,0:T(8,128)(2,1)S(1)}, u32[]{:S(2)}, u32[]{:S(2)}) %collective-permute-start.7) | collective-permute-done | bytes 589856 | tf_op jit(solution)/shard_map/ppermute | solution.py:281
  108.6 0.8 copy-done.11
  109.7 14.7 %shard_map.70 = bf16[2,4,128,512]{3,2,1,0:T(8,128)(2,1)} custom-call(s32[34,2]{1,0:T(8,128)} %copy.8.shift, s32[4]{0:T(128)} %left_size.5, s32[4]{0:T(128)} %right_size.5, bf16[2,4,256,128]{3,2,1,0:T(8,128)(2,1)} %copy-done.5, bf16[2,4,256,128]{3,2,1,0:T(8,128)(2,1)} %copy-done.3, bf16[2,4,256,128]{3,2,1,0:T(8,128)(2,1)} %copy-done.4, ...), custom_call_target="tpu_custom_call" | custom-call | flops 4831838208 | bytes 10485760 | tf_op jit(solution)/shard_map/pallas_call | solution.py:243
  (68 shorter events, 4.7 us)
Async XLA Ops:
  3.3 76.4 %copy-start.3 = (bf16[2,4,256,128]{3,2,1,0:T(8,128)(2,1)}, bf16[2,4,256,128]{3,2,1,0:T(8,128)(2,1)S(1)}, u32[]{:S(2)}) copy-start(bf16[2,4,256,128]{3,2,1,0:T(8,128)(2,1)S(1)} %get-tuple-element.12.down) | copy-start | bytes 1572868
  3.4 76.4 %copy-start.4 = (bf16[2,4,256,128]{3,2,1,0:T(8,128)(2,1)}, bf16[2,4,256,128]{3,2,1,0:T(8,128)(2,1)S(1)}, u32[]{:S(2)}) copy-start(bf16[2,4,256,128]{3,2,1,0:T(8,128)(2,1)S(1)} %get-tuple-element.11.up) | copy-start | bytes 1572868
  3.4 35.9 %collective-permute-start = (bf16[2,4,256,128]{3,2,1,0:T(8,128)(2,1)S(1)}, bf16[2,4,256,128]{3,2,1,0:T(8,128)(2,1)S(1)}, u32[]{:S(2)}, u32[]{:S(2)}) collective-permute-start(bf16[2,4,256,128]{3,2,1,0:T(8,128)(2,1)S(1)} %get-tuple-element.11.up), channel_id=1, source_target_pairs={{0,1},{1,2},{2,3},{3,4},{4,5},{5,6},{6,7},{7,8},{8,9},{9,10},{10,1... | collective-permute-start | bytes 1572872 | tf_op jit(solution)/shard_map/ppermute | solution.py:268
  8.8 12.4 %collective-permute-start.17 = (bf16[16,4,8,128]{3,2,1,0:T(8,128)(2,1)S(1)}, bf16[16,4,8,128]{3,2,1,0:T(8,128)(2,1)S(1)}, u32[]{:S(2)}, u32[]{:S(2)}) collective-permute-start(bf16[16,4,8,128]{3,2,1,0:T(8,128)(2,1)S(1)} %get-tuple-element.16.own), channel_id=1, source_target_pairs={{0,1},{1,2},{2,3},{3,0},{4,5},{5,6},{6,7},{7,4},{8,9},{9,10},{10,1... | collective-permute-start | bytes 393224 | tf_op jit(solution)/shard_map/ppermute | solution.py:260
  10.4 17.5 %collective-permute-start.18 = (bf16[16,4,8,128]{3,2,1,0:T(8,128)(2,1)S(1)}, bf16[16,4,8,128]{3,2,1,0:T(8,128)(2,1)S(1)}, u32[]{:S(2)}, u32[]{:S(2)}) collective-permute-start(bf16[16,4,8,128]{3,2,1,0:T(8,128)(2,1)S(1)} %get-tuple-element.16.own), channel_id=1, source_target_pairs={{0,3},{1,0},{2,1},{3,2},{4,7},{5,4},{6,5},{7,6},{8,11},{9,8},{10,9... | collective-permute-start | bytes 393224 | tf_op jit(solution)/shard_map/ppermute | solution.py:260
  11.5 17.7 %collective-permute-start.19 = (bf16[16,4,8,128]{3,2,1,0:T(8,128)(2,1)S(1)}, bf16[16,4,8,128]{3,2,1,0:T(8,128)(2,1)S(1)}, u32[]{:S(2)}, u32[]{:S(2)}) collective-permute-start(bf16[16,4,8,128]{3,2,1,0:T(8,128)(2,1)S(1)} %get-tuple-element.16.own), channel_id=1, source_target_pairs={{0,2},{1,3},{2,0},{3,1},{4,6},{5,7},{6,4},{7,5},{8,10},{9,11},{10,... | collective-permute-start | bytes 393224 | tf_op jit(solution)/shard_map/ppermute | solution.py:260
  13.6 17.2 %collective-permute-start.4 = (bf16[18,4,8,128]{3,2,1,0:T(8,128)(2,1)S(1)}, bf16[18,4,8,128]{3,2,1,0:T(8,128)(2,1)S(1)}, u32[]{:S(2)}, u32[]{:S(2)}) collective-permute-start(bf16[18,4,8,128]{3,2,1,0:T(8,128)(2,1)S(1)} %get-tuple-element.15.own), channel_id=1, source_target_pairs={{0,4},{1,5},{2,6},{3,7},{4,8},{5,9},{6,10},{7,11},{8,12},{9,13},{1... | collective-permute-start | bytes 442376 | tf_op jit(solution)/shard_map/ppermute | solution.py:261
  21.1 11.0 %collective-permute-start.5 = (bf16[18,4,8,128]{3,2,1,0:T(8,128)(2,1)S(1)}, bf16[18,4,8,128]{3,2,1,0:T(8,128)(2,1)S(1)}, u32[]{:S(2)}, u32[]{:S(2)}) collective-permute-start(bf16[18,4,8,128]{3,2,1,0:T(8,128)(2,1)S(1)} %get-tuple-element.15.own), channel_id=1, source_target_pairs={{0,12},{1,13},{2,14},{3,15},{4,0},{5,1},{6,2},{7,3},{8,4},{9,5},{1... | collective-permute-start | bytes 442376 | tf_op jit(solution)/shard_map/ppermute | solution.py:261
  27.9 24.7 %collective-permute-start.10 = (bf16[34,4,16,128]{3,2,1,0:T(8,128)(2,1)}, bf16[34,4,16,128]{3,2,1,0:T(8,128)(2,1)S(1)}, u32[]{:S(2)}, u32[]{:S(2)}) collective-permute-start(bf16[34,4,16,128]{3,2,1,0:T(8,128)(2,1)} %rights_0_.3), channel_id=1, source_target_pairs={{0,32},{16,48},{32,64},{48,80},{64,96},{80,112},{96,0},{112,16},{1... | collective-permute-start | bytes 1671176 | tf_op jit(solution)/shard_map/ppermute | solution.py:258
  29.2 25.3 %collective-permute-start.11 = (bf16[34,4,16,128]{3,2,1,0:T(8,128)(2,1)}, bf16[34,4,16,128]{3,2,1,0:T(8,128)(2,1)S(1)}, u32[]{:S(2)}, u32[]{:S(2)}) collective-permute-start(bf16[34,4,16,128]{3,2,1,0:T(8,128)(2,1)} %rights_0_.3), channel_id=1, source_target_pairs={{0,96},{16,112},{32,0},{48,16},{64,32},{80,48},{96,64},{112,80},{1... | collective-permute-start | bytes 1671176 | tf_op jit(solution)/shard_map/ppermute | solution.py:258
  30.7 52.7 %copy-start.10 = (s32[34,2]{0,1:T(2,128)S(1)}, s32[34,2]{0,1:T(2,128)}, u32[]{:S(2)}) copy-start(s32[34,2]{0,1:T(2,128)} %param.11) | copy-start | bytes 820
  30.7 13.7 %collective-permute-start.1 = (bf16[2,4,256,128]{3,2,1,0:T(8,128)(2,1)S(1)}, bf16[2,4,256,128]{3,2,1,0:T(8,128)(2,1)S(1)}, u32[]{:S(2)}, u32[]{:S(2)}) collective-permute-start(bf16[2,4,256,128]{3,2,1,0:T(8,128)(2,1)S(1)} %get-tuple-element.12.down), channel_id=1, source_target_pairs={{1,0},{2,1},{3,2},{4,3},{5,4},{6,5},{7,6},{8,7},{9,8},{10,9},{11,1... | collective-permute-start | bytes 1572872 | tf_op jit(solution)/shard_map/ppermute | solution.py:269
  32.2 6.0 %collective-permute-start.6 = (bf16[18,4,8,128]{3,2,1,0:T(8,128)(2,1)S(1)}, bf16[18,4,8,128]{3,2,1,0:T(8,128)(2,1)S(1)}, u32[]{:S(2)}, u32[]{:S(2)}) collective-permute-start(bf16[18,4,8,128]{3,2,1,0:T(8,128)(2,1)S(1)} %get-tuple-element.15.own), channel_id=1, source_target_pairs={{0,8},{1,9},{2,10},{3,11},{4,12},{5,13},{6,14},{7,15},{8,0},{9,1},... | collective-permute-start | bytes 442376 | tf_op jit(solution)/shard_map/ppermute | solution.py:261
  38.1 19.0 %collective-permute-start.12 = (bf16[34,4,16,128]{3,2,1,0:T(8,128)(2,1)}, bf16[34,4,16,128]{3,2,1,0:T(8,128)(2,1)S(1)}, u32[]{:S(2)}, u32[]{:S(2)}) collective-permute-start(bf16[34,4,16,128]{3,2,1,0:T(8,128)(2,1)} %rights_0_.3), channel_id=1, source_target_pairs={{0,64},{16,80},{32,96},{48,112},{64,0},{80,16},{96,32},{112,48},{1... | collective-permute-start | bytes 1671176 | tf_op jit(solution)/shard_map/ppermute | solution.py:258
  39.3 40.4 %copy-start.5 = (bf16[2,4,256,128]{3,2,1,0:T(8,128)(2,1)}, bf16[2,4,256,128]{3,2,1,0:T(8,128)(2,1)S(1)}, u32[]{:S(2)}) copy-start(bf16[2,4,256,128]{3,2,1,0:T(8,128)(2,1)S(1)} %collective-permute-done.low_r) | copy-start | bytes 1572868
  39.3 20.9 %collective-permute-start.13 = (bf16[34,4,16,128]{3,2,1,0:T(8,128)(2,1)}, bf16[34,4,16,128]{3,2,1,0:T(8,128)(2,1)S(1)}, u32[]{:S(2)}, u32[]{:S(2)}) collective-permute-start(bf16[34,4,16,128]{3,2,1,0:T(8,128)(2,1)} %rights_0_.3), channel_id=1, source_target_pairs={{0,16},{16,0},{32,48},{48,32},{64,80},{80,64},{96,112},{112,96},{1... | collective-permute-start | bytes 1671176 | tf_op jit(solution)/shard_map/ppermute | solution.py:278
  42.5 41.7 %copy-start.2 = (bf16[4,16,4,8,128]{4,3,2,1,0:T(8,128)(2,1)}, bf16[4,16,4,8,128]{4,3,2,1,0:T(8,128)(2,1)S(1)}, u32[]{:S(2)}) copy-start(bf16[4,16,4,8,128]{4,3,2,1,0:T(8,128)(2,1)S(1)} %shard_map.68.lefts_0_) | copy-start | bytes 1572868
  44.4 39.7 %copy-start.6 = (bf16[2,4,256,128]{3,2,1,0:T(8,128)(2,1)}, bf16[2,4,256,128]{3,2,1,0:T(8,128)(2,1)S(1)}, u32[]{:S(2)}) copy-start(bf16[2,4,256,128]{3,2,1,0:T(8,128)(2,1)S(1)} %collective-permute-done.1.high_r) | copy-start | bytes 1572868
  44.4 22.3 %collective-permute-start.20 = (bf16[4,16,4,8,128]{4,3,2,1,0:T(8,128)(2,1)S(1)}, bf16[4,16,4,8,128]{4,3,2,1,0:T(8,128)(2,1)S(1)}, u32[]{:S(2)}, u32[]{:S(2)}) collective-permute-start(bf16[4,16,4,8,128]{4,3,2,1,0:T(8,128)(2,1)S(1)} %shard_map.68.lefts_0_), channel_id=1, source_target_pairs={{0,4},{1,5},{2,6},{3,7},{4,8},{5,9},{6,10},{7,11},{8,12},{9,13},{1... | collective-permute-start | bytes 1572872 | tf_op jit(solution)/shard_map/ppermute | solution.py:272
  52.6 29.9 %copy-start.13 = (bf16[34,4,16,128]{3,2,1,0:T(8,128)(2,1)}, bf16[34,4,16,128]{3,2,1,0:T(8,128)(2,1)S(1)}, u32[]{:S(2)}) copy-start(bf16[34,4,16,128]{3,2,1,0:T(8,128)(2,1)S(1)} %collective-permute-done.10.rights_1_) | copy-start | bytes 1671172
  52.6 14.6 %collective-permute-start.21 = (bf16[4,16,4,8,128]{4,3,2,1,0:T(8,128)(2,1)S(1)}, bf16[4,16,4,8,128]{4,3,2,1,0:T(8,128)(2,1)S(1)}, u32[]{:S(2)}, u32[]{:S(2)}) collective-permute-start(bf16[4,16,4,8,128]{4,3,2,1,0:T(8,128)(2,1)S(1)} %shard_map.68.lefts_0_), channel_id=1, source_target_pairs={{0,12},{1,13},{2,14},{3,15},{4,0},{5,1},{6,2},{7,3},{8,4},{9,5},{1... | collective-permute-start | bytes 1572872 | tf_op jit(solution)/shard_map/ppermute | solution.py:272
  54.5 28.1 %copy-start.14 = (bf16[34,4,16,128]{3,2,1,0:T(8,128)(2,1)}, bf16[34,4,16,128]{3,2,1,0:T(8,128)(2,1)S(1)}, u32[]{:S(2)}) copy-start(bf16[34,4,16,128]{3,2,1,0:T(8,128)(2,1)S(1)} %collective-permute-done.11.rights_2_) | copy-start | bytes 1671172
  54.5 24.3 %collective-permute-start.22 = (bf16[4,16,4,8,128]{4,3,2,1,0:T(8,128)(2,1)S(1)}, bf16[4,16,4,8,128]{4,3,2,1,0:T(8,128)(2,1)S(1)}, u32[]{:S(2)}, u32[]{:S(2)}) collective-permute-start(bf16[4,16,4,8,128]{4,3,2,1,0:T(8,128)(2,1)S(1)} %shard_map.68.lefts_0_), channel_id=1, source_target_pairs={{0,8},{1,9},{2,10},{3,11},{4,12},{5,13},{6,14},{7,15},{8,0},{9,1},... | collective-permute-start | bytes 1572872 | tf_op jit(solution)/shard_map/ppermute | solution.py:272
  57.1 25.4 %copy-start.15 = (bf16[34,4,16,128]{3,2,1,0:T(8,128)(2,1)}, bf16[34,4,16,128]{3,2,1,0:T(8,128)(2,1)S(1)}, u32[]{:S(2)}) copy-start(bf16[34,4,16,128]{3,2,1,0:T(8,128)(2,1)S(1)} %collective-permute-done.12.rights_3_) | copy-start | bytes 1671172
  57.1 27.0 %collective-permute-start.2 = (bf16[8,2,256,128]{3,2,1,0:T(8,128)(2,1)}, bf16[8,2,256,128]{3,2,1,0:T(8,128)(2,1)}, u32[]{:S(2)}, u32[]{:S(2)}) collective-permute-start(bf16[8,2,256,128]{3,2,1,0:T(8,128)(2,1)} %get-tuple-element.13), channel_id=1, source_target_pairs={{0,16},{16,32},{32,48},{48,64},{64,80},{80,96},{96,112},{1,17},{17... | collective-permute-start | bytes 3145736 | tf_op jit(solution)/shard_map/ppermute | solution.py:274
  60.2 23.9 %collective-permute-start.3 = (bf16[8,2,256,128]{3,2,1,0:T(8,128)(2,1)}, bf16[8,2,256,128]{3,2,1,0:T(8,128)(2,1)}, u32[]{:S(2)}, u32[]{:S(2)}) collective-permute-start(bf16[8,2,256,128]{3,2,1,0:T(8,128)(2,1)} %get-tuple-element.14), channel_id=1, source_target_pairs={{16,0},{32,16},{48,32},{64,48},{80,64},{96,80},{112,96},{17,1},{33... | collective-permute-start | bytes 3145736 | tf_op jit(solution)/shard_map/ppermute | solution.py:275
  66.7 13.1 %collective-permute-start.14 = (bf16[34,4,16,128]{3,2,1,0:T(8,128)(2,1)S(1)}, bf16[34,4,16,128]{3,2,1,0:T(8,128)(2,1)S(1)}, u32[]{:S(2)}, u32[]{:S(2)}) collective-permute-start(bf16[34,4,16,128]{3,2,1,0:T(8,128)(2,1)S(1)} %collective-permute-done.10.rights_1_), channel_id=1, source_target_pairs={{0,16},{16,0},{32,48},{48,32},{64,80},{80,64},{96,112},{112,96},{1... | collective-permute-start | bytes 1671176 | tf_op jit(solution)/shard_map/ppermute | solution.py:278
  67.3 12.6 %collective-permute-start.15 = (bf16[34,4,16,128]{3,2,1,0:T(8,128)(2,1)S(1)}, bf16[34,4,16,128]{3,2,1,0:T(8,128)(2,1)S(1)}, u32[]{:S(2)}, u32[]{:S(2)}) collective-permute-start(bf16[34,4,16,128]{3,2,1,0:T(8,128)(2,1)S(1)} %collective-permute-done.11.rights_2_), channel_id=1, source_target_pairs={{0,16},{16,0},{32,48},{48,32},{64,80},{80,64},{96,112},{112,96},{1... | collective-permute-start | bytes 1671176 | tf_op jit(solution)/shard_map/ppermute | solution.py:278
  78.8 3.7 %collective-permute-start.16 = (bf16[34,4,16,128]{3,2,1,0:T(8,128)(2,1)S(1)}, bf16[34,4,16,128]{3,2,1,0:T(8,128)(2,1)S(1)}, u32[]{:S(2)}, u32[]{:S(2)}) collective-permute-start(bf16[34,4,16,128]{3,2,1,0:T(8,128)(2,1)S(1)} %collective-permute-done.12.rights_3_), channel_id=1, source_target_pairs={{0,16},{16,0},{32,48},{48,32},{64,80},{80,64},{96,112},{112,96},{1... | collective-permute-start | bytes 1671176 | tf_op jit(solution)/shard_map/ppermute | solution.py:278
  79.8 28.8 %collective-permute-start.7 = (bf16[4,18,4,8,128]{4,3,2,1,0:T(8,128)(2,1)S(1)}, bf16[4,18,4,8,128]{4,3,2,1,0:T(8,128)(2,1)S(1)}, u32[]{:S(2)}, u32[]{:S(2)}) collective-permute-start(bf16[4,18,4,8,128]{4,3,2,1,0:T(8,128)(2,1)S(1)} %shard_map.67.lefts_0_), channel_id=1, source_target_pairs={{0,1},{1,2},{2,3},{3,0},{4,5},{5,6},{6,7},{7,4},{8,9},{9,10},{10,1... | collective-permute-start | bytes 1769480 | tf_op jit(solution)/shard_map/ppermute | solution.py:281
  79.9 28.7 %collective-permute-start.8 = (bf16[4,18,4,8,128]{4,3,2,1,0:T(8,128)(2,1)S(1)}, bf16[4,18,4,8,128]{4,3,2,1,0:T(8,128)(2,1)S(1)}, u32[]{:S(2)}, u32[]{:S(2)}) collective-permute-start(bf16[4,18,4,8,128]{4,3,2,1,0:T(8,128)(2,1)S(1)} %shard_map.67.lefts_0_), channel_id=1, source_target_pairs={{0,3},{1,0},{2,1},{3,2},{4,7},{5,4},{6,5},{7,6},{8,11},{9,8},{10,9... | collective-permute-start | bytes 1769480 | tf_op jit(solution)/shard_map/ppermute | solution.py:281
  83.4 25.2 %collective-permute-start.9 = (bf16[4,18,4,8,128]{4,3,2,1,0:T(8,128)(2,1)S(1)}, bf16[4,18,4,8,128]{4,3,2,1,0:T(8,128)(2,1)}, u32[]{:S(2)}, u32[]{:S(2)}) collective-permute-start(bf16[4,18,4,8,128]{4,3,2,1,0:T(8,128)(2,1)S(1)} %shard_map.67.lefts_0_), channel_id=1, source_target_pairs={{0,2},{1,3},{2,0},{3,1},{4,6},{5,7},{6,4},{7,5},{8,10},{9,11},{10,... | collective-permute-start | bytes 1769480 | tf_op jit(solution)/shard_map/ppermute | solution.py:281
  (14 other events, 86.9 us)
